TPU v7x, 32 devices: a whole 2x2x4 slice. The times are simulated.
32 devices in a mesh: dp: 2 (over core), ctx: 16 (over z, y, x).
Axes of the slice: x: 2, y: 2, z: 4, core: 2. Of those that a mesh axis runs over, the one named last changes fastest.
Arguments:
- layer_input: bfloat16 [2, 2048, 16384], P('dp', 'ctx'), may hold values from -6 to 6
- query_rows: bfloat16 [2, 2048, 1024], P('dp', 'ctx'), may hold values from -512 to 512
- key_rows: bfloat16 [2, 2048, 128], P('dp', 'ctx'), may hold values from -5 to 5
- value_rows: bfloat16 [2, 2048, 128], P('dp', 'ctx'), may hold values from -6 to 6
- out_grad: bfloat16 [2, 2048, 1024], P('dp', 'ctx'), may hold values from -6 to 6
- block_order: int32 [32], replicated, may hold values from 0 to 31, each once
- master: float32 [16384, 1280], P(('dp', 'ctx')), may hold values from -3 to 3
- moment_one: float32 [16384, 1280], P(('dp', 'ctx')), may hold values from -6 to 6
- moment_two: float32 [16384, 1280], P(('dp', 'ctx')), may hold values from 0.5 to 20
Outputs:
- new_master: float32 [16384, 1280], P(('dp', 'ctx'))
- new_moment_one: float32 [16384, 1280], P(('dp', 'ctx'))
- new_moment_two: float32 [16384, 1280], P(('dp', 'ctx'))
Inputs may be any that keep to these rules, and one draw needn't show every extreme that they name: Stored rows j * 64 to (j + 1) * 64 - 1 of every sequence hold positions block_order[j] * 64 onward, in order; each of the 32 blocks appears once.
All inputs are finite; a program needn't handle non-finite values.
Results may differ from a plain program's by a relative error of at most 0.0048.
Values may be sent and summed in bfloat16 or wider, within the bound.
No kernel may reach another device: no remote copies, remote signals or barrier semaphores. Data moves between devices by JAX's collectives and lax.ppermute only.
A program may use at most 64 MiB of HBM per device.

v0:
```python
import math

import jax
import jax.numpy as jnp
from jax import lax
from jax.sharding import PartitionSpec as P

STEP = 10


NEG_FILL = -1e30
BETA_ONE = 0.9
BETA_TWO = 0.95
EPSILON = 1e-08
LEARN_RATE = 0.01
DECAY = 0.1
ROW_CONTRACT = (((1,), (1,)), ((), ()))
COL_CONTRACT = (((0,), (0,)), ((), ()))


def forward_block(carried, key_blk, value_blk, key_pos, rows_q, rows_o, query_pos, score_scale):
    max_old, total_old, inner_old = carried
    scores = (
        lax.dot_general(rows_q, key_blk, ROW_CONTRACT, preferred_element_type=jnp.float32)
        * score_scale
    )
    grad_prob = lax.dot_general(rows_o, value_blk, ROW_CONTRACT, preferred_element_type=jnp.float32)
    visible = key_pos[None, :] <= query_pos[:, None]
    max_new = jnp.maximum(max_old, jnp.max(jnp.where(visible, scores, NEG_FILL), axis=1))
    weights = jnp.where(visible, jnp.exp(scores - max_new[:, None]), 0.0)
    factor = jnp.exp(max_old - max_new)
    return (
        max_new,
        total_old * factor + jnp.sum(weights, axis=1),
        inner_old * factor + jnp.sum(weights * grad_prob, axis=1),
    )


def forward_over(
    carried, key_all, value_all, key_pos_all, rows_q, rows_o, query_pos, score_scale, block_size
):
    key_count = key_all.shape[0]
    blk_rows = math.gcd(key_count, block_size)
    blk_count = key_count // blk_rows

    def forward_advance(state_now, block_items):
        key_blk, value_blk, key_pos = block_items
        return (
            forward_block(
                state_now, key_blk, value_blk, key_pos, rows_q, rows_o, query_pos, score_scale
            ),
            None,
        )

    result, unused_out = lax.scan(
        forward_advance,
        carried,
        (
            key_all.reshape(blk_count, blk_rows, -1),
            value_all.reshape(blk_count, blk_rows, -1),
            key_pos_all.reshape(blk_count, blk_rows),
        ),
    )
    return result


def backward_over(
    key_all, value_all, key_pos_all, rows_q, rows_o, query_pos, log_total, delta_row, score_scale
):
    key_count, head_dim = key_all.shape
    blk_rows = math.gcd(key_count, 512)
    blk_count = key_count // blk_rows

    def backward_advance(dq_acc, block_items):
        key_blk, value_blk, key_pos = block_items
        scores = (
            lax.dot_general(rows_q, key_blk, ROW_CONTRACT, preferred_element_type=jnp.float32)
            * score_scale
        )
        visible = key_pos[None, :] <= query_pos[:, None]
        prob_full = jnp.where(visible, jnp.exp(scores - log_total[:, None]), 0.0)
        grad_prob = lax.dot_general(
            rows_o, value_blk, ROW_CONTRACT, preferred_element_type=jnp.float32
        )
        dscore = (prob_full * (grad_prob - delta_row[:, None]) * score_scale).astype(jnp.bfloat16)
        prob_low = prob_full.astype(jnp.bfloat16)
        acc_out = dq_acc + jnp.dot(dscore, key_blk, preferred_element_type=jnp.float32)
        key_term = lax.dot_general(dscore, rows_q, COL_CONTRACT, preferred_element_type=jnp.float32)
        value_term = lax.dot_general(
            prob_low, rows_o, COL_CONTRACT, preferred_element_type=jnp.float32
        )
        return (acc_out, jnp.concatenate([key_term, value_term], axis=1))

    start_acc = jnp.zeros((rows_q.shape[0], head_dim), jnp.float32)
    dq_final, key_terms = lax.scan(
        backward_advance,
        start_acc,
        (
            key_all.reshape(blk_count, blk_rows, -1),
            value_all.reshape(blk_count, blk_rows, -1),
            key_pos_all.reshape(blk_count, blk_rows),
        ),
    )
    return (dq_final, key_terms.reshape(key_count, 2 * head_dim))


def per_device(
    layer_input,
    query_rows,
    key_rows,
    value_rows,
    out_grad,
    block_order,
    master,
    moment_one,
    moment_two,
):
    tok_rows = query_rows.shape[1]
    q_width = query_rows.shape[2]
    head_dim = key_rows.shape[2]
    group_size = q_width // head_dim
    half_rows = tok_rows // 2
    block_count = block_order.shape[0]
    seq_length = block_count * half_rows
    dp_count = lax.axis_size("dp")
    ctx_count = lax.axis_size("ctx")
    own_rows = master.shape[0]
    score_scale = 1.0 / math.sqrt(head_dim)
    pos_all = (
        block_order[:, None] * half_rows + jnp.arange(half_rows, dtype=jnp.int32)[None, :]
    ).reshape(seq_length)
    ctx_rank = lax.axis_index("ctx")
    my_pos = lax.dynamic_slice_in_dim(pos_all, ctx_rank * tok_rows, tok_rows)
    query_pos = jnp.repeat(my_pos, group_size)
    rows_q = query_rows[0].reshape(tok_rows * group_size, head_dim)
    rows_o = out_grad[0].reshape(tok_rows * group_size, head_dim)
    keys_here = key_rows[0]
    values_here = value_rows[0]
    pieces = layer_input[0].reshape(tok_rows, dp_count, ctx_count, own_rows)
    received = lax.all_to_all(pieces, "ctx", split_axis=2, concat_axis=0, tiled=True)
    columns = received.reshape(seq_length, dp_count * own_rows)
    row_total = tok_rows * group_size
    start_state = (
        jnp.full((row_total,), NEG_FILL, jnp.float32),
        jnp.zeros((row_total,), jnp.float32),
        jnp.zeros((row_total,), jnp.float32),
    )
    fold_size = 512
    max_run, total_run, inner_run = forward_over(
        start_state,
        lax.all_gather(keys_here, "ctx", axis=0, tiled=True),
        lax.all_gather(values_here, "ctx", axis=0, tiled=True),
        pos_all,
        rows_q,
        rows_o,
        query_pos,
        score_scale,
        fold_size,
    )
    key_all, value_all = (
        lax.all_gather(keys_here, "ctx", axis=0, tiled=True),
        lax.all_gather(values_here, "ctx", axis=0, tiled=True),
    )
    log_total = max_run + jnp.log(total_run)
    delta_row = inner_run / total_run
    dq_final, key_terms = backward_over(
        key_all, value_all, pos_all, rows_q, rows_o, query_pos, log_total, delta_row, score_scale
    )
    dq_local = dq_final.astype(jnp.bfloat16).reshape(tok_rows, q_width)
    kv_full = lax.psum(key_terms, "ctx").astype(jnp.bfloat16)
    dq_all = lax.all_gather(dq_local, "ctx", axis=0, tiled=True)
    query_part = lax.dot_general(columns, dq_all, COL_CONTRACT, preferred_element_type=jnp.float32)
    key_part = lax.dot_general(columns, kv_full, COL_CONTRACT, preferred_element_type=jnp.float32)
    grad_local = lax.psum_scatter(
        jnp.concatenate([query_part, key_part], axis=1), "dp", scatter_dimension=0, tiled=True
    )
    new_one = BETA_ONE * moment_one + (1.0 - BETA_ONE) * grad_local
    new_two = BETA_TWO * moment_two + (1.0 - BETA_TWO) * grad_local * grad_local
    corr_one = 1.0 - BETA_ONE**STEP
    corr_two = 1.0 - BETA_TWO**STEP
    update = new_one / corr_one / (jnp.sqrt(new_two / corr_two) + EPSILON)
    new_master = master - LEARN_RATE * (update + DECAY * master)
    return (new_master, new_one, new_two)


def solution(mesh):
    in_specs = (
        P("dp", "ctx", None),
        P("dp", "ctx", None),
        P("dp", "ctx", None),
        P("dp", "ctx", None),
        P("dp", "ctx", None),
        P(),
        P(("dp", "ctx"), None),
        P(("dp", "ctx"), None),
        P(("dp", "ctx"), None),
    )
    out_specs = (P(("dp", "ctx"), None), P(("dp", "ctx"), None), P(("dp", "ctx"), None))
    return jax.shard_map(
        per_device, mesh=mesh, in_specs=in_specs, out_specs=out_specs, check_vma=False
    )
```

profile of v0, /device:TPU:0, one launch (start us, length us, event | category | flops | bytes accessed | tf_op | source)
XLA Modules:
  0.0 409.1 jit_solution(8991061759737383845)
XLA Ops:
  7.2 6.4 %copy.38 = bf16[1,128,16384]{1,2,0:T(8,128)(2,1)} copy(bf16[1,128,16384]{2,1,0:T(8,128)(2,1)} %param.13) | data formatting | bytes 8388608 | tf_op args[0]
  13.6 4.6 %copy.39 = bf16[128,2,16,512]{0,3,1,2:T(8,128)(2,1)} copy(bf16[128,2,16,512]{0,3,2,1:T(8,128)(2,1)} %bitcast.121) | data formatting | bytes 8388608 | tf_op jit(solution)/shard_map/reshape;squeeze | solution.py:139
  18.2 8.5 %all-to-all-start = ((bf16[128,2,16,512]{0,3,1,2:T(8,128)(2,1)}), bf16[128,2,16,512]{0,3,1,2:T(8,128)(2,1)}, u32[]{:S(2)}, u32[]{:S(2)}) async-start(bf16[128,2,16,512]{0,3,1,2:T(8,128)(2,1)} %copy.39), calls=%async_computation | async-start | bytes 8388608 | tf_op jit(solution)/shard_map/all_to_all | solution.py:140
  27.3 114.0 %all-gather = bf16[1,2048,128]{2,1,0:T(8,128)(2,1)} all-gather(bf16[1,128,128]{2,1,0:T(8,128)(2,1)S(1)} %copy-done.4), channel_id=2, replica_groups=mesh['dp'=2,'ctx'=16] {'ctx'}, dimensions={1}, use_global_device_ids=true | all-gather | bytes 557056 | tf_op jit(solution)/shard_map/all_gather | solution.py:161
  141.3 50.5 %all-gather.1 = bf16[1,2048,128]{2,1,0:T(8,128)(2,1)} all-gather(bf16[1,128,128]{2,1,0:T(8,128)(2,1)S(1)} %copy-done.5), channel_id=3, replica_groups=mesh['dp'=2,'ctx'=16] {'ctx'}, dimensions={1}, use_global_device_ids=true | all-gather | bytes 557056 | tf_op jit(solution)/shard_map/all_gather | solution.py:162
  192.1 14.9 %while.28 = (s32[]{:T(128)}, f32[1024]{0:T(1024)S(1)}, f32[1024]{0:T(1024)S(1)}, f32[1024]{0:T(1024)S(1)}, s32[4,512]{1,0:T(4,128)S(1)}, /*index=5*/bf16[4,512,1...) while((s32[]{:T(128)}, f32[1024]{0:T(1024)S(1)}, ...), condition=%wide.region_4.5_spmd.clone, body=%wide.region_0.4_spmd.clone.sunk | while | flops 276306944 | bytes 7188100 | solution.py:55
  194.2 1.6 fusion.81
  198.0 1.6 fusion.81
  201.7 1.6 fusion.81
  205.4 1.6 fusion.81
  207.1 26.5 %while.29 = (s32[]{:T(128)}, f32[1024,128]{1,0:T(8,128)S(1)}, f32[4,512,256]{2,1,0:T(8,128)}, s32[4,512]{1,0:T(4,128)S(1)}, bf16[4,512,128]{2,1,0:T(8,128)(2,1)}...) while((s32[]{:T(128)}, f32[1024,128]{1,0:T(8,128)S(1)}, ...), condition=%wide.region_6.7_spmd.clone, body=%wide.region_5.6_spmd.clone.sunk | while | flops 676200448 | bytes 15630987 | solution.py:95
  207.3 1.5 bitcast_select_fusion.2
  212.2 1.5 convolution_add_fusion.2
  213.9 1.5 bitcast_select_fusion.2
  218.8 1.5 convolution_add_fusion.2
  220.5 1.5 bitcast_select_fusion.2
  225.5 1.5 convolution_add_fusion.2
  227.2 1.5 bitcast_select_fusion.2
  232.1 1.5 convolution_add_fusion.2
  234.5 118.5 %all-reduce.1 = bf16[2048,256]{1,0:T(8,128)(2,1)S(1)} all-reduce(f32[2048,256]{1,0:T(8,128)} %bitcast.126), channel_id=1, replica_groups=mesh['dp'=2,'ctx'=16] {'ctx'}, use_global_device_ids=true, to_apply=%region_7.8 | all-reduce | flops 524288 | bytes 3145728 | tf_op jit(solution)/shard_map/psum | solution.py:170
  353.0 4.9 %copy.40 = bf16[16,128,2,1,512]{1,0,4,2,3:T(8,128)(2,1)S(1)} copy(bf16[16,128,2,1,512]{1,4,2,0,3:T(8,128)(2,1)} %bitcast.4) | data formatting | bytes 8388608 | tf_op jit(solution)/shard_map/all_to_all | solution.py:140
  357.9 1.9 copy-done.1
  361.2 7.7 %fusion.37 = f32[1024,1024]{0,1:T(8,128)S(1)} fusion(bf16[2048,1024]{1,0:T(8,128)(2,1)} %all-gather.4.cloned.1.call-done, bf16[128,8,16,128]{3,2,1,0:T(8,128)(2,1)} %bitcast.123), kind=kOutput, calls=%fused_computation.54 | convolution fusion | flops 4294967296 | bytes 12582912 | tf_op jit(solution)/shard_map/dot_general | solution.py:172
  368.9 3.1 pad_maximum_fusion
  372.1 2.2 copy.37
  374.2 3.2 copy.42
  377.5 3.8 copy.44
  381.2 4.4 %reduce-scatter.2.cloned.1.call-done = f32[512,1280]{0,1:T(8,128)} async-done(((f32[1024,1280]{0,1:T(8,128)}), f32[512,1280]{0,1:T(8,128)}) %reduce-scatter.2.cloned.1.call-update) | async-done | bytes 2621456 | tf_op jit(solution)/shard_map/reduce_scatter | solution.py:174
  385.6 8.0 %multiply_subtract_fusion = (f32[512,1280]{0,1:T(8,128)}, f32[512,1280]{0,1:T(8,128)}, f32[512,1280]{0,1:T(8,128)}) fusion(f32[512,1280]{0,1:T(8,128)} %copy.44, f32[512,1280]{0,1:T(8,128)} %reduce-scatter.2.cloned.1.call-done, f32[512,1280]{0,1:T(8,128)S(1)} %copy.37, f32[512,1280]{0,1:T(8,128)} %copy.42), kind=kLoop, calls=%fused_computation.52 | loop fusion | flops 9830400 | bytes 18350080 | tf_op jit(solution)/shard_map/sub | solution.py:182
  393.6 3.2 copy.45
  396.8 3.4 copy.46
  400.1 2.1 copy.47
  (108 shorter events, 25.6 us)
Async XLA Ops:
  18.2 8.6 %copy-start.6 = (s32[32]{0:T(128)S(1)}, s32[32]{0:T(128)}, u32[]{:S(2)}) copy-start(s32[32]{0:T(128)} %param.18) | copy-start | bytes 388
  18.2 9.1 %copy-start.4 = (bf16[1,128,128]{2,1,0:T(8,128)(2,1)S(1)}, bf16[1,128,128]{2,1,0:T(8,128)(2,1)}, u32[]{:S(2)}) copy-start(bf16[1,128,128]{2,1,0:T(8,128)(2,1)} %param.15) | copy-start | bytes 98308
  18.2 123.1 %copy-start.5 = (bf16[1,128,128]{2,1,0:T(8,128)(2,1)S(1)}, bf16[1,128,128]{2,1,0:T(8,128)(2,1)}, u32[]{:S(2)}) copy-start(bf16[1,128,128]{2,1,0:T(8,128)(2,1)} %param.16) | copy-start | bytes 98308
  18.2 173.6 %copy-start.2 = (bf16[1,128,1024]{2,1,0:T(8,128)(2,1)S(1)}, bf16[1,128,1024]{2,1,0:T(8,128)(2,1)}, u32[]{:S(2)}) copy-start(bf16[1,128,1024]{2,1,0:T(8,128)(2,1)} %param.17) | copy-start | bytes 786436
  18.2 173.7 %copy-start.3 = (bf16[1,128,1024]{2,1,0:T(8,128)(2,1)S(1)}, bf16[1,128,1024]{2,1,0:T(8,128)(2,1)}, u32[]{:S(2)}) copy-start(bf16[1,128,1024]{2,1,0:T(8,128)(2,1)} %param.14) | copy-start | bytes 786436
  18.2 334.8 %all-to-all-start = ((bf16[128,2,16,512]{0,3,1,2:T(8,128)(2,1)}), bf16[128,2,16,512]{0,3,1,2:T(8,128)(2,1)}, u32[]{:S(2)}, u32[]{:S(2)}) async-start(bf16[128,2,16,512]{0,3,1,2:T(8,128)(2,1)} %copy.39), calls=%async_computation | async-start | bytes 8388608 | tf_op jit(solution)/shard_map/all_to_all | solution.py:140
  26.7 334.4 %all-gather.4.cloned.1.call-start = ((), (), s32[]{:S(2)}) async-start(), calls=%async_computation.2 | async-start | bytes 4456448 | tf_op jit(solution)/shard_map/all_gather | solution.py:171
  234.5 151.1 %reduce-scatter.2.cloned.1.call-start = ((), (), s32[]{:S(2)}) async-start(), calls=%async_computation.3 | async-start | bytes 7864320 | tf_op jit(solution)/shard_map/reduce_scatter | solution.py:174
  357.9 1.9 copy-start.1
  396.8 3.4 copy-start
Sparse Core Ops, SparseCore 0:
  234.6 103.9 all-gather.3
  372.2 13.3 reduce-scatter.1
where the time goes:
time: 410 us; the launch traced here: 409 us
  blocking collectives  283 us (69%)
  local copies, waits for them, and re-layouts  42.7 us (10%)
  matrix products  42 us (10%)
  between operations  14.2 us (3%)
  other arithmetic  13.5 us (3%)
  starting transfers between devices  8.62 us (2%)
  waiting for transfers between devices  4.42 us (1%)
    psum x1, blocking collectives, per_device(): kv_full = lax.psum(key_terms, 'ctx').astype(jnp.bfloat16)  118 us
    all_gather x1, blocking collectives, per_device(): lax.all_gather(keys_here, 'ctx', axis=0, tiled=True)  114 us
    all_gather x1, blocking collectives, per_device(): lax.all_gather(values_here, 'ctx', axis=0, tiled=True)  50.5 us
    unnamed x21, local copies, waits for them, and re-layouts  26.2 us
    all_to_all x1, starting transfers between devices, per_device(): lax.all_to_all(pieces, 'ctx', split_axis=2, concat_axis=0, tiled=True)  8.54 us
  transfers between devices with their start and end apart: 3, of which 1 were waited for; matrix products, arithmetic and copies ran while one was open for 14% of the time, Pallas kernels for 0%

commit v1 on v0

v1 whole, which is shorter than its diff:
```python
import functools
import math

import jax
import jax.numpy as jnp
from jax import lax
from jax.experimental import pallas as pl
from jax.experimental.pallas import tpu as pltpu
from jax.sharding import PartitionSpec as P


STEP = 10
BETA_ONE = 0.9
BETA_TWO = 0.95
EPSILON = 1e-08
LEARN_RATE = 0.01
DECAY = 0.1
NEG_FILL = -1e30
LOG2E = 1.4426950408889634
ROW_CONTRACT = (((1,), (1,)), ((), ()))
F32 = jnp.float32
BF16 = jnp.bfloat16


def swap(block, mask, count):
    return lax.ppermute(block, "ctx", [(i, i ^ mask) for i in range(count)])


def stage_bits(count):
    bits = []
    bit = count // 2
    while bit >= 4:
        bits.append(bit)
        bit //= 2
    return bits


def slot_order(count):
    order = [0]
    for bit in stage_bits(count):
        order = order + [o ^ bit for o in order]
    return order


def fan_out(held, count, relay=False):
    parts = [held] + [swap(held, j, count) for j in range(1, 3)]
    if not relay:
        return parts + [swap(held, 3, count)]
    half = held.shape[1] // 2
    left = swap(parts[1][:, :half], 2, count)
    right = swap(parts[2][:, half:], 1, count)
    return parts + [(left, right)]


def spread(block, count, relay=False):
    held = block
    for bit in stage_bits(count):
        held = jnp.concatenate([held, swap(held, bit, count)], axis=0)
    return fan_out(held, count, relay)


def total_terms(parts, count):
    total = parts[0].astype(F32)
    for j in range(1, 4):
        other = swap(parts[j], j, count)
        total = total + other.astype(F32)
    tok = total.shape[0] // (count // 4)
    order = slot_order(count)
    for bit in stage_bits(count):
        other = swap(total.astype(BF16), bit, count)
        blocks = [other[order.index(o ^ bit) * tok :][:tok] for o in order]
        total = total + jnp.concatenate(blocks, axis=0).astype(F32)
    return total.astype(BF16)


def pack_kernel(masks, dp_count, ctx_count, me_ref, x_ref, *refs):
    outs = refs[: len(masks)]
    held_ref, sem = refs[len(masks) :]
    own = held_ref.shape[2]
    copies = []
    for i, mask in enumerate(masks):
        for d in range(dp_count):
            first = pl.multiple_of((d * ctx_count + (me_ref[0] ^ mask)) * own, 128)
            at = i * dp_count + d
            copies.append(
                pltpu.make_async_copy(
                    x_ref.at[:, pl.ds(first, own)], held_ref.at[at], sem.at[at]
                )
            )
    for copy in copies:
        copy.start()
    for i, out_ref in enumerate(outs):
        for d in range(dp_count):
            at = i * dp_count + d
            copies[at].wait()
            out_ref[d * own : (d + 1) * own, :] = held_ref[at].T


def pack(rows, me, masks, dp_count, ctx_count, own):
    tok = rows.shape[0]
    count = len(masks)
    if own % 128:
        slabs = rows.T.reshape(dp_count, ctx_count, own, tok).transpose(1, 0, 2, 3)
        slabs = slabs.reshape(ctx_count, dp_count * own, tok)
        return [lax.dynamic_index_in_dim(slabs, me[0] ^ mask, 0, False) for mask in masks]
    return pl.pallas_call(
        functools.partial(pack_kernel, masks, dp_count, ctx_count),
        in_specs=[
            pl.BlockSpec(memory_space=pltpu.SMEM),
            pl.BlockSpec(memory_space=pltpu.HBM),
        ],
        out_specs=[pl.BlockSpec(memory_space=pltpu.VMEM)] * count,
        out_shape=[jax.ShapeDtypeStruct((dp_count * own, tok), rows.dtype)] * count,
        scratch_shapes=[
            pltpu.VMEM((count * dp_count, tok, own), rows.dtype),
            pltpu.SemaphoreType.DMA((count * dp_count,)),
        ],
        compiler_params=pltpu.CompilerParams(vmem_limit_bytes=8 << 20),
        cost_estimate=pl.CostEstimate(
            flops=0, bytes_accessed=4 * count * dp_count * own * tok, transcendentals=0
        ),
        name="pack_rows",
    )(me, pltpu.with_memory_space_constraint(rows, pltpu.HBM))


def attention_kernel(order, me_ref, blocks_ref, q_ref, o_ref, *refs):
    kv_refs = refs[:4]
    dq_ref = refs[4]
    dkv_refs = refs[5:9]
    s_ref, g_ref, kt_ref, acc_ref = refs[9:]
    step = pl.program_id(0)
    tok, pair = q_ref.shape
    head_dim = pair // 2
    half = tok // 2
    rows = kv_refs[0].shape[0]
    me = me_ref[0]
    scale = 1.0 / math.sqrt(head_dim)

    @pl.when(step == 0)
    def _():
        acc_ref[...] = jnp.zeros_like(acc_ref)
        for j in range(4):
            kt_ref[:, j * rows : (j + 1) * rows] = kv_refs[j][:, :head_dim].T

    q2 = jnp.concatenate([q_ref[:, :head_dim], q_ref[:, head_dim:]], axis=0)
    o2 = jnp.concatenate([o_ref[:, :head_dim], o_ref[:, head_dim:]], axis=0)
    lane = lax.broadcasted_iota(jnp.int32, (1, 2 * tok), 1)
    lane = jnp.where(lane >= tok, lane - tok, lane)
    first = blocks_ref[2 * me]
    second = blocks_ref[2 * me + 1]
    query_pos = jnp.where(lane < half, first * half + lane, second * half + lane - half)
    in_block = lax.broadcasted_iota(jnp.int32, (half, 2 * tok), 0)

    top = jnp.full((1, 2 * tok), NEG_FILL, F32)
    for j in range(4):
        scores = lax.dot_general(
            kv_refs[j][:, :head_dim], q2, ROW_CONTRACT, preferred_element_type=F32
        )
        for i, o in enumerate(order):
            for u in range(2):
                lo = i * tok + u * half
                key_base = blocks_ref[2 * (me ^ (o ^ j)) + u] * half
                part = scores[lo : lo + half] * (scale * LOG2E)
                part = jnp.where(in_block <= query_pos - key_base, part, NEG_FILL)
                s_ref[j * rows + lo : j * rows + lo + half, :] = part
                top = jnp.maximum(top, jnp.max(part, axis=0, keepdims=True))
    denom = jnp.zeros((1, 2 * tok), F32)
    inner = jnp.zeros((1, 2 * tok), F32)
    for j in range(4):
        grads = lax.dot_general(
            kv_refs[j][:, head_dim:], o2, ROW_CONTRACT, preferred_element_type=F32
        )
        g_ref[j * rows : (j + 1) * rows, :] = grads
        for lo in range(0, rows, half):
            at = slice(j * rows + lo, j * rows + lo + half)
            weight = jnp.exp2(s_ref[at, :] - top)
            s_ref[at, :] = weight
            denom = denom + jnp.sum(weight, axis=0, keepdims=True)
            inner = inner + jnp.sum(weight * grads[lo : lo + half], axis=0, keepdims=True)
    inv = 1.0 / denom
    delta = inner * inv
    dqt = jnp.zeros((head_dim, 2 * tok), F32)
    for j in range(4):
        at = slice(j * rows, (j + 1) * rows)
        prob = s_ref[at, :] * inv
        ds = (prob * (g_ref[at, :] - delta) * scale).astype(BF16)
        prob = prob.astype(BF16)
        acc_ref[at, :head_dim] += jnp.dot(ds, q2, preferred_element_type=F32)
        acc_ref[at, head_dim:] += jnp.dot(prob, o2, preferred_element_type=F32)
        dqt = dqt + jnp.dot(kt_ref[:, at], ds, preferred_element_type=F32)
    dq2 = dqt.T.astype(BF16)
    dq_ref[:, :head_dim] = dq2[:tok]
    dq_ref[:, head_dim:] = dq2[tok:]

    @pl.when(step == pl.num_programs(0) - 1)
    def _():
        for j in range(4):
            dkv_refs[j][...] = acc_ref[j * rows : (j + 1) * rows, :].astype(BF16)


def attention(me, blocks, q, o, kv_parts, order):
    tok, width = q.shape
    rows, kv_width = kv_parts[0].shape
    head_dim = kv_width // 2
    pair = 2 * head_dim
    flops = 2 * 5 * tok * (width // head_dim) * 4 * rows * head_dim
    row_spec = pl.BlockSpec((tok, pair), lambda g, *_: (0, g))
    kv_spec = pl.BlockSpec((rows, kv_width), lambda g, *_: (0, 0))
    outs = pl.pallas_call(
        functools.partial(attention_kernel, order),
        grid_spec=pltpu.PrefetchScalarGridSpec(
            num_scalar_prefetch=2,
            grid=(width // pair,),
            in_specs=[row_spec, row_spec] + [kv_spec] * 4,
            out_specs=[row_spec] + [kv_spec] * 4,
            scratch_shapes=[
                pltpu.VMEM((4 * rows, 2 * tok), F32),
                pltpu.VMEM((4 * rows, 2 * tok), F32),
                pltpu.VMEM((head_dim, 4 * rows), BF16),
                pltpu.VMEM((4 * rows, kv_width), F32),
            ],
        ),
        out_shape=[jax.ShapeDtypeStruct((tok, width), BF16)]
        + [jax.ShapeDtypeStruct((rows, kv_width), BF16)] * 4,
        compiler_params=pltpu.CompilerParams(vmem_limit_bytes=16 << 20),
        cost_estimate=pl.CostEstimate(
            flops=flops, bytes_accessed=4 * 2 * rows * kv_width * 2, transcendentals=0
        ),
        name="attention",
    )(me, blocks, q, o, *kv_parts)
    return outs[0], list(outs[1:])


def grad_kernel(halves, slots, slab_ref, *refs):
    x_refs, refs = refs[:slots], list(refs[slots:])
    out_ref, xs_ref = refs[-2:]
    dq_refs = []
    for count in halves:
        dq_refs.append(refs[:count])
        del refs[:count]
    dkv_refs = refs[: len(halves)]
    acc_refs = refs[len(halves) : -2]
    own = xs_ref.shape[0]
    tok = x_refs[0].shape[1]
    rows, tile = dkv_refs[0].shape
    rows_at = pl.ds(pl.multiple_of(slab_ref[0] * own, own), own)
    for i, x_ref in enumerate(x_refs):
        xs_ref[:, i * tok : (i + 1) * tok] = x_ref[rows_at, :]

    def put(parts, columns):
        out = None
        for j, part in enumerate(parts):
            term = jnp.dot(xs_ref[:, j * rows : (j + 1) * rows], part, preferred_element_type=F32)
            out = term if out is None else out + term
        for ref in acc_refs:
            out = out + ref[:, columns]
        out_ref[:, columns] = out.astype(out_ref.dtype)

    def run(side, first, count):
        def step(t, _):
            to = pl.multiple_of(first + t * tile, tile)
            parts = []
            for pair in dq_refs:
                split = len(pair) == 2
                at = pl.multiple_of(t * tile, tile) if split else to
                parts.append(pair[side if split else 0][:, pl.ds(at, tile)])
            put(parts, pl.ds(to, tile))
            return 0

        lax.fori_loop(0, count, step, 0, unroll=True)

    half = (out_ref.shape[1] - tile) // 2
    run(0, 0, half // tile)
    run(1, half, half // tile)
    put([ref[...] for ref in dkv_refs], pl.ds(2 * half, tile))


def grad_call(groups, slab, kind, acc=()):
    xs = [block for group in groups for block in group[0]]
    dqs = [group[1] if isinstance(group[1], tuple) else (group[1],) for group in groups]
    dkvs = [group[2] for group in groups]
    tok = xs[0].shape[1]
    own = xs[0].shape[0] // lax.axis_size("dp")
    width = sum(half.shape[1] for half in dqs[0]) + dkvs[0].shape[1]
    operands = xs + [half for halves in dqs for half in halves] + dkvs + list(acc)
    in_place = pl.BlockSpec(memory_space=pltpu.VMEM)
    return pl.pallas_call(
        functools.partial(grad_kernel, [len(halves) for halves in dqs], len(xs)),
        in_specs=[pl.BlockSpec(memory_space=pltpu.SMEM)] + [in_place] * len(operands),
        out_specs=in_place,
        out_shape=jax.ShapeDtypeStruct((own, width), kind),
        scratch_shapes=[pltpu.VMEM((own, len(xs) * tok), BF16)],
        compiler_params=pltpu.CompilerParams(vmem_limit_bytes=16 << 20),
        cost_estimate=pl.CostEstimate(
            flops=2 * len(xs) * tok * own * width,
            bytes_accessed=sum(x.size * x.dtype.itemsize for x in operands),
            transcendentals=0,
        ),
        name="weight_grad",
    )(slab, *operands)


def update_kernel(others, tile, grad_ref, *refs):
    other_refs, state = refs[:others], refs[others : others + 3]
    outs, held, sem = refs[others + 3 : others + 6], refs[others + 6 : others + 9], refs[-1]
    inv_one = 1.0 / (1.0 - BETA_ONE**STEP)
    inv_two = 1.0 / (1.0 - BETA_TWO**STEP)

    def step(t, _):
        columns = pl.ds(pl.multiple_of(t * tile, tile), tile)
        grad = grad_ref[:, columns]
        for ref in other_refs:
            grad = grad + ref[:, columns].astype(F32)
        master, one, two = (ref[:, columns] for ref in state)
        new_one = BETA_ONE * one + (1.0 - BETA_ONE) * grad
        new_two = BETA_TWO * two + (1.0 - BETA_TWO) * grad * grad
        update = (new_one * inv_one) / (jnp.sqrt(new_two * inv_two) + EPSILON)
        held[0][:, columns] = master - LEARN_RATE * (update + DECAY * master)
        held[1][:, columns] = new_one
        held[2][:, columns] = new_two
        for i in range(3):
            pltpu.make_async_copy(
                held[i].at[:, columns], outs[i].at[:, columns], sem.at[i]
            ).start()
        return 0

    lax.fori_loop(0, grad_ref.shape[1] // tile, step, 0)
    for i in range(3):
        pltpu.make_async_copy(held[i], outs[i], sem.at[i]).wait()


def update_call(grad, others, state, tile):
    in_place = pl.BlockSpec(memory_space=pltpu.VMEM)
    return pl.pallas_call(
        functools.partial(update_kernel, len(others), tile),
        in_specs=[in_place] * (4 + len(others)),
        out_specs=[pl.BlockSpec(memory_space=pl.ANY)] * 3,
        out_shape=[jax.ShapeDtypeStruct(grad.shape, F32)] * 3,
        scratch_shapes=[pltpu.VMEM(grad.shape, F32)] * 3 + [pltpu.SemaphoreType.DMA((3,))],
        compiler_params=pltpu.CompilerParams(vmem_limit_bytes=16 << 20),
        cost_estimate=pl.CostEstimate(
            flops=20 * grad.size, bytes_accessed=28 * grad.size, transcendentals=grad.size
        ),
        name="weight_update",
    )(grad, *others, *state)


def per_device(
    layer_input,
    query_rows,
    key_rows,
    value_rows,
    out_grad,
    block_order,
    master,
    moment_one,
    moment_two,
):
    dp_count = lax.axis_size("dp")
    ctx_count = lax.axis_size("ctx")
    own_rows = master.shape[0]
    order = slot_order(ctx_count)
    me = lax.axis_index("ctx").astype(jnp.int32).reshape(1)
    dp_rank = lax.axis_index("dp").astype(jnp.int32)

    x_groups = []
    for j in range(4):
        masks = tuple(o ^ j for o in order)
        packed = pack(layer_input[0], me, masks, dp_count, ctx_count, own_rows)
        blocks = []
        for i, o in enumerate(order):
            block = packed[i]
            blocks.append(block if o ^ j == 0 else swap(block, o ^ j, ctx_count))
        x_groups.append(blocks)

    kv_parts = spread(jnp.concatenate([key_rows[0], value_rows[0]], axis=1), ctx_count)
    dq, dkv_terms = attention(me, block_order, query_rows[0], out_grad[0], kv_parts, order)
    dq_parts = spread(dq, ctx_count, relay=True)
    dkv_parts = fan_out(total_terms(dkv_terms, ctx_count), ctx_count)
    groups = list(zip(x_groups, dq_parts, dkv_parts))

    slabs = [lax.rem(dp_rank + k, dp_count).reshape(1) for k in range(dp_count)]
    most = []
    for k in range(dp_count):
        most.append(grad_call(groups[:3], slabs[k], F32))
    received = []
    for k in range(1, dp_count):
        part = grad_call(groups[3:], slabs[k], BF16, most[k : k + 1])
        received.append(
            lax.ppermute(part, "dp", [(i, (i + k) % dp_count) for i in range(dp_count)])
        )
    grad = grad_call(groups[3:], slabs[0], F32, most[:1])
    state = (master, moment_one, moment_two)
    return tuple(update_call(grad, received, state, 2 * key_rows.shape[2]))


def solution(mesh):
    in_specs = (
        P("dp", "ctx", None),
        P("dp", "ctx", None),
        P("dp", "ctx", None),
        P("dp", "ctx", None),
        P("dp", "ctx", None),
        P(),
        P(("dp", "ctx"), None),
        P(("dp", "ctx"), None),
        P(("dp", "ctx"), None),
    )
    out_specs = (P(("dp", "ctx"), None), P(("dp", "ctx"), None), P(("dp", "ctx"), None))

    return jax.shard_map(
        per_device, mesh=mesh, in_specs=in_specs, out_specs=out_specs, check_vma=False
    )
```

time: 410 us -> 235 us (0.57)
  blocking collectives: 283 us -> 0 us
  starting transfers between devices: 8.62 us -> 84.3 us
  waiting for transfers between devices: 4.42 us -> 72.3 us
  matrix products: 42 us -> 0 us
  Pallas kernels: 0 us -> 33.7 us
  between operations: 14.2 us -> 1.19 us
  other arithmetic: 13.5 us -> 2.93 us
    all_gather x2 -> x0, blocking collectives: 165 us -> none  [the longest x1 114 us: per_device(): lax.all_gather(keys_here, 'ctx', axis=0, tiled=True)]
    psum x1 -> x0, blocking collectives: 118 us -> none  [per_device(): kv_full = lax.psum(key_terms, 'ctx').astype(jnp.bfloat16)]
    ppermute x0 -> x35, starting transfers between devices: none -> 84.3 us  [the longest x34 84.3 us: swap(): return lax.ppermute(block, 'ctx', [(i, i ^ mask) for i in range(count)])]
    ppermute x0 -> x35, waiting for transfers between devices: none -> 72.3 us  [the longest x34 72.3 us: swap(): return lax.ppermute(block, 'ctx', [(i, i ^ mask) for i in range(count)])]
    dot_general x30 -> x0, matrix products: 42 us -> none  [the longest x1 7.71 us: per_device(): lax.dot_general(columns, dq_all, COL_CONTRACT, preferred_element_type=jnp...]
    pallas_call x0 -> x10, Pallas kernels: none -> 33.7 us  [the longest x1 11 us: attention(): pl.pallas_call(functools.partial(attention_kernel, order), grid_spec=pltp...]
    unnamed x21 -> x110, local copies, waits for them, and re-layouts: 26.2 us -> 37.5 us
    all_to_all x1 -> x0, starting transfers between devices: 8.54 us -> none  [per_device(): lax.all_to_all(pieces, 'ctx', split_axis=2, concat_axis=0, tiled=True)]
  transfers between devices with their start and end apart: 3 -> 35, of which waited for: 1 -> 12; matrix products, arithmetic and copies ran while one was open for 14% -> 1% of each run, Pallas kernels for 0% -> 6%
where the time goes in v1:
time: 235 us; the launch traced here: 234 us
  starting transfers between devices  84.3 us (36%)
  waiting for transfers between devices  72.3 us (31%)
  local copies, waits for them, and re-layouts  39.2 us (17%)
  Pallas kernels  33.7 us (14%)
  other arithmetic  2.93 us (1%)
    ppermute x34, starting transfers between devices, swap(): return lax.ppermute(block, 'ctx', [(i, i ^ mask) for i in range(count)])  84.3 us
    ppermute x34, waiting for transfers between devices, swap(): return lax.ppermute(block, 'ctx', [(i, i ^ mask) for i in range(count)])  72.3 us
    unnamed x110, local copies, waits for them, and re-layouts  37.5 us
    pallas_call x1, Pallas kernels, attention(): pl.pallas_call(functools.partial(attention_kernel, order), grid_spec=pltp...  11 us
    pallas_call x4, Pallas kernels, grad_call(): pl.pallas_call(functools.partial(grad_kernel, [len(halves) for halves in...  10.3 us
    pallas_call x4, Pallas kernels, pack(): pl.pallas_call(functools.partial(pack_kernel, masks, dp_count, ctx_count)...  7.46 us
    pallas_call x1, Pallas kernels, update_call(): pl.pallas_call(functools.partial(update_kernel, len(others), tile), in_sp...  4.9 us
  transfers between devices with their start and end apart: 35, of which 12 were waited for; matrix products, arithmetic and copies ran while one was open for 1% of the time, Pallas kernels for 6%

profile of v1, /device:TPU:0, one launch (start us, length us, event | category | flops | bytes accessed | tf_op | source)
XLA Modules:
  0.0 233.6 jit_solution(17128029801314735454)
XLA Ops:
  1.4 4.1 %collective-permute-start.4 = (bf16[128,256]{1,0:T(8,128)(2,1)S(1)}, bf16[128,256]{1,0:T(8,128)(2,1)S(1)}, u32[]{:S(2)}, u32[]{:S(2)}) collective-permute-start(bf16[128,256]{1,0:T(8,128)(2,1)S(1)} %pad_maximum_fusion.4), channel_id=1, source_target_pairs={{0,8},{1,9},{2,10},{3,11},{4,12},{5,13},{6,14},{7,15},{8,0},{9,1},... | collective-permute-start | bytes 196616 | tf_op jit(solution)/shard_map/ppermute | solution.py:26
  5.5 3.6 %collective-permute-done.4 = bf16[128,256]{1,0:T(8,128)(2,1)S(1)} collective-permute-done((bf16[128,256]{1,0:T(8,128)(2,1)S(1)}, bf16[128,256]{1,0:T(8,128)(2,1)S(1)}, u32[]{:S(2)}, u32[]{:S(2)}) %collective-permute-start.4) | collective-permute-done | bytes 65568 | tf_op jit(solution)/shard_map/ppermute | solution.py:26
  10.6 4.4 %collective-permute-done.5 = bf16[256,256]{1,0:T(8,128)(2,1)S(1)} collective-permute-done((bf16[256,256]{1,0:T(8,128)(2,1)S(1)}, bf16[256,256]{1,0:T(8,128)(2,1)S(1)}, u32[]{:S(2)}, u32[]{:S(2)}) %collective-permute-start.5) | collective-permute-done | bytes 131104 | tf_op jit(solution)/shard_map/ppermute | solution.py:26
  19.4 4.8 %collective-permute-done.6.refs_1_ = bf16[512,256]{1,0:T(8,128)(2,1)S(1)} collective-permute-done((bf16[512,256]{1,0:T(8,128)(2,1)S(1)}, bf16[512,256]{1,0:T(8,128)(2,1)S(1)}, u32[]{:S(2)}, u32[]{:S(2)}) %collective-permute-start.6) | collective-permute-done | bytes 262176 | tf_op jit(solution)/shard_map/ppermute | solution.py:26
  24.1 4.1 %collective-permute-done.7.refs_2_ = bf16[512,256]{1,0:T(8,128)(2,1)S(1)} collective-permute-done((bf16[512,256]{1,0:T(8,128)(2,1)S(1)}, bf16[512,256]{1,0:T(8,128)(2,1)S(1)}, u32[]{:S(2)}, u32[]{:S(2)}) %collective-permute-start.7) | collective-permute-done | bytes 262176 | tf_op jit(solution)/shard_map/ppermute | solution.py:26
  30.8 11.0 %attention.1 = (bf16[128,1024]{1,0:T(8,128)(2,1)S(1)}, bf16[512,256]{1,0:T(8,128)(2,1)S(1)}, bf16[512,256]{1,0:T(8,128)(2,1)S(1)}, bf16[512,256]{1,0:T(8,128)(2,1)S(1)}, bf16[512,256]{1,0:T(8,128)(2,1)S(1)}) custom-call(s32[1]{0:T(128)} %bitcast.1.me_ref, s32[32]{0:T(128)S(1)} %copy-done.53, bf16[128,1024]{1,0:T(8,128)(2,1)S(1)} %bitcast.8, ...), custom_call_target="tpu_custom_call" | custom-call | flops 2684354560 | bytes 2097152 | tf_op jit(solution)/shard_map/attention/pallas_call | solution.py:209
  41.7 4.2 %collective-permute-start.9 = (bf16[128,1024]{1,0:T(8,128)(2,1)S(1)}, bf16[128,1024]{1,0:T(8,128)(2,1)S(1)}, u32[]{:S(2)}, u32[]{:S(2)}) collective-permute-start(bf16[128,1024]{1,0:T(8,128)(2,1)S(1)} %get-tuple-element.28), channel_id=1, source_target_pairs={{0,8},{1,9},{2,10},{3,11},{4,12},{5,13},{6,14},{7,15},{8,0},{9,1},... | collective-permute-start | bytes 786440 | tf_op jit(solution)/shard_map/ppermute | solution.py:26
  45.9 10.1 %collective-permute-done.9 = bf16[128,1024]{1,0:T(8,128)(2,1)S(1)} collective-permute-done((bf16[128,1024]{1,0:T(8,128)(2,1)S(1)}, bf16[128,1024]{1,0:T(8,128)(2,1)S(1)}, u32[]{:S(2)}, u32[]{:S(2)}) %collective-permute-start.9) | collective-permute-done | bytes 262176 | tf_op jit(solution)/shard_map/ppermute | solution.py:26
  59.0 3.4 %collective-permute-start.21 = (bf16[1024,128]{1,0:T(8,128)(2,1)S(1)}, bf16[1024,128]{1,0:T(8,128)(2,1)S(1)}, u32[]{:S(2)}, u32[]{:S(2)}) collective-permute-start(bf16[1024,128]{1,0:T(8,128)(2,1)S(1)} %get-tuple-element.34), channel_id=1, source_target_pairs={{0,8},{1,9},{2,10},{3,11},{4,12},{5,13},{6,14},{7,15},{8,0},{9,1},... | collective-permute-start | bytes 786440 | tf_op jit(solution)/shard_map/ppermute | solution.py:26
  65.9 9.1 %collective-permute-done.10 = bf16[256,1024]{1,0:T(8,128)(2,1)S(1)} collective-permute-done((bf16[256,1024]{1,0:T(8,128)(2,1)S(1)}, bf16[256,1024]{1,0:T(8,128)(2,1)S(1)}, u32[]{:S(2)}, u32[]{:S(2)}) %collective-permute-start.10) | collective-permute-done | bytes 524320 | tf_op jit(solution)/shard_map/ppermute | solution.py:26
  75.1 3.6 %collective-permute-start.23 = (bf16[1024,128]{1,0:T(8,128)(2,1)S(1)}, bf16[1024,128]{1,0:T(8,128)(2,1)S(1)}, u32[]{:S(2)}, u32[]{:S(2)}) collective-permute-start(bf16[1024,128]{1,0:T(8,128)(2,1)S(1)} %get-tuple-element.36), channel_id=1, source_target_pairs={{0,12},{1,13},{2,14},{3,15},{4,8},{5,9},{6,10},{7,11},{8,4},{9,5},... | collective-permute-start | bytes 786440 | tf_op jit(solution)/shard_map/ppermute | solution.py:26
  83.4 6.7 %collective-permute-start.25 = (bf16[1024,128]{1,0:T(8,128)(2,1)S(1)}, bf16[1024,128]{1,0:T(8,128)(2,1)S(1)}, u32[]{:S(2)}, u32[]{:S(2)}) collective-permute-start(bf16[1024,128]{1,0:T(8,128)(2,1)S(1)} %get-tuple-element.38), channel_id=1, source_target_pairs={{0,9},{1,8},{2,11},{3,10},{4,13},{5,12},{6,15},{7,14},{8,1},{9,0},... | collective-permute-start | bytes 786440 | tf_op jit(solution)/shard_map/ppermute | solution.py:26
  92.4 13.0 %collective-permute-start.26 = (bf16[1024,128]{1,0:T(8,128)(2,1)S(1)}, bf16[1024,128]{1,0:T(8,128)(2,1)S(1)}, u32[]{:S(2)}, u32[]{:S(2)}) collective-permute-start(bf16[1024,128]{1,0:T(8,128)(2,1)S(1)} %get-tuple-element.39), channel_id=1, source_target_pairs={{0,5},{1,4},{2,7},{3,6},{4,1},{5,0},{6,3},{7,2},{8,13},{9,12},{10,... | collective-permute-start | bytes 786440 | tf_op jit(solution)/shard_map/ppermute | solution.py:26
  105.5 3.5 %collective-permute-done.18 = bf16[512,256]{1,0:T(8,128)(2,1)S(1)} collective-permute-done((bf16[512,256]{1,0:T(8,128)(2,1)S(1)}, bf16[512,256]{1,0:T(8,128)(2,1)S(1)}, u32[]{:S(2)}, u32[]{:S(2)}) %collective-permute-start.18) | collective-permute-done | bytes 262176 | tf_op jit(solution)/shard_map/ppermute | solution.py:26
  109.0 13.0 %collective-permute-done.24.refs_4_ = bf16[1024,128]{1,0:T(8,128)(2,1)S(1)} collective-permute-done((bf16[1024,128]{1,0:T(8,128)(2,1)S(1)}, bf16[1024,128]{1,0:T(8,128)(2,1)S(1)}, u32[]{:S(2)}, u32[]{:S(2)}) %collective-permute-start.24) | collective-permute-done | bytes 262176 | tf_op jit(solution)/shard_map/ppermute | solution.py:26
  123.7 2.4 %pack_rows.4 = (bf16[1024,128]{1,0:T(8,128)(2,1)S(1)}, bf16[1024,128]{1,0:T(8,128)(2,1)S(1)}, bf16[1024,128]{1,0:T(8,128)(2,1)}, bf16[1024,128]{1,0:T(8,128)(2,1)}) custom-call(s32[1]{0:T(128)} %bitcast.1.me_ref, bf16[128,16384]{1,0:T(8,128)(2,1)} %bitcast.13), custom_call_target="tpu_custom_call" | custom-call | bytes 2097152 | tf_op jit(solution)/shard_map/pack_rows/pallas_call | solution.py:106
  126.1 5.9 %collective-permute-done.27.refs_7_ = bf16[1024,128]{1,0:T(8,128)(2,1)S(1)} collective-permute-done((bf16[1024,128]{1,0:T(8,128)(2,1)S(1)}, bf16[1024,128]{1,0:T(8,128)(2,1)S(1)}, u32[]{:S(2)}, u32[]{:S(2)}) %collective-permute-start.27) | collective-permute-done | bytes 262176 | tf_op jit(solution)/shard_map/ppermute | solution.py:26
  132.0 4.1 %collective-permute-start.29 = (bf16[1024,128]{1,0:T(8,128)(2,1)S(1)}, bf16[1024,128]{1,0:T(8,128)(2,1)S(1)}, u32[]{:S(2)}, u32[]{:S(2)}) collective-permute-start(bf16[1024,128]{1,0:T(8,128)(2,1)S(1)} %get-tuple-element.42), channel_id=1, source_target_pairs={{0,10},{1,11},{2,8},{3,9},{4,14},{5,15},{6,12},{7,13},{8,2},{9,3},... | collective-permute-start | bytes 786440 | tf_op jit(solution)/shard_map/ppermute | solution.py:26
  136.1 4.2 %collective-permute-done.28.refs_8_ = bf16[1024,128]{1,0:T(8,128)(2,1)S(1)} collective-permute-done((bf16[1024,128]{1,0:T(8,128)(2,1)S(1)}, bf16[1024,128]{1,0:T(8,128)(2,1)S(1)}, u32[]{:S(2)}, u32[]{:S(2)}) %collective-permute-start.28) | collective-permute-done | bytes 262176 | tf_op jit(solution)/shard_map/ppermute | solution.py:26
  140.3 6.3 %collective-permute-start.30 = (bf16[1024,128]{1,0:T(8,128)(2,1)S(1)}, bf16[1024,128]{1,0:T(8,128)(2,1)S(1)}, u32[]{:S(2)}, u32[]{:S(2)}) collective-permute-start(bf16[1024,128]{1,0:T(8,128)(2,1)S(1)} %get-tuple-element.43), channel_id=1, source_target_pairs={{0,6},{1,7},{2,4},{3,5},{4,2},{5,3},{6,0},{7,1},{8,14},{9,15},{10,... | collective-permute-start | bytes 786440 | tf_op jit(solution)/shard_map/ppermute | solution.py:26
  146.6 4.1 %collective-permute-start.31 = (bf16[1024,128]{1,0:T(8,128)(2,1)S(1)}, bf16[1024,128]{1,0:T(8,128)(2,1)S(1)}, u32[]{:S(2)}, u32[]{:S(2)}) collective-permute-start(bf16[1024,128]{1,0:T(8,128)(2,1)S(1)} %get-tuple-element.44), channel_id=1, source_target_pairs={{0,14},{1,15},{2,12},{3,13},{4,10},{5,11},{6,8},{7,9},{8,6},{9,7},... | collective-permute-start | bytes 786440 | tf_op jit(solution)/shard_map/ppermute | solution.py:26
  150.7 4.5 %collective-permute-start = (bf16[1024,128]{1,0:T(8,128)(2,1)S(1)}, bf16[1024,128]{1,0:T(8,128)(2,1)S(1)}, u32[]{:S(2)}, u32[]{:S(2)}) collective-permute-start(bf16[1024,128]{1,0:T(8,128)(2,1)S(1)} %get-tuple-element.24), channel_id=1, source_target_pairs={{0,3},{1,2},{2,1},{3,0},{4,7},{5,6},{6,5},{7,4},{8,11},{9,10},{10,... | collective-permute-start | bytes 786440 | tf_op jit(solution)/shard_map/ppermute | solution.py:26
  159.8 2.3 collective-permute-start.33
  162.8 2.3 collective-permute-start.12
  165.8 2.9 %collective-permute-start.14 = (bf16[512,512]{1,0:T(8,128)(2,1)}, bf16[512,512]{1,0:T(8,128)(2,1)}, u32[]{:S(2)}, u32[]{:S(2)}) collective-permute-start(bf16[512,512]{1,0:T(8,128)(2,1)} %slice.45), channel_id=1, source_target_pairs={{0,1},{1,0},{2,3},{3,2},{4,5},{5,4},{6,7},{7,6},{8,9},{9,8},{10,11... | collective-permute-start | bytes 1572872 | tf_op jit(solution)/shard_map/ppermute | solution.py:26
  172.3 8.5 %collective-permute-done.32.refs_16_ = bf16[512,256]{1,0:T(8,128)(2,1)S(1)} collective-permute-done((bf16[512,256]{1,0:T(8,128)(2,1)S(1)}, bf16[512,256]{1,0:T(8,128)(2,1)S(1)}, u32[]{:S(2)}, u32[]{:S(2)}) %collective-permute-start.32) | collective-permute-done | bytes 262176 | tf_op jit(solution)/shard_map/ppermute | solution.py:26
  182.2 8.7 %collective-permute-start.20 = (bf16[512,256]{1,0:T(8,128)(2,1)S(1)}, bf16[512,256]{1,0:T(8,128)(2,1)}, u32[]{:S(2)}, u32[]{:S(2)}) collective-permute-start(bf16[512,256]{1,0:T(8,128)(2,1)S(1)} %add_convert_fusion.refs_15_), channel_id=1, source_target_pairs={{0,3},{1,2},{2,1},{3,0},{4,7},{5,6},{6,5},{7,4},{8,11},{9,10},{10,... | collective-permute-start | bytes 786440 | tf_op jit(solution)/shard_map/ppermute | solution.py:26
  204.1 2.2 weight_grad.6.refs_7_
  206.4 3.4 %weight_grad.7 = bf16[512,1280]{1,0:T(8,128)(2,1)} custom-call(s32[1]{0:T(128)} %bitcast.7.slab_ref, bf16[1024,128]{1,0:T(8,128)(2,1)S(1)} %copy-done.40, bf16[1024,128]{1,0:T(8,128)(2,1)S(1)} %copy-done.43, bf16[1024,128]{1,0:T(8,128)(2,1)} %collective-permute-done.2.refs_2_, bf16[1024,128]{1,0:T(8,128)(2,1)} %collective-permute-done.3.refs_3_, ...), custom_call_target="tpu_custom_call" | custom-call | flops 671088640 | bytes 4980736 | tf_op jit(solution)/shard_map/weight_grad/pallas_call | solution.py:287
  223.1 2.3 weight_grad.4.refs_7_
  225.4 2.5 %weight_grad.5.grad_ref = f32[512,1280]{1,0:T(8,128)S(1)} custom-call(s32[1]{0:T(128)} %bitcast.slab_ref, bf16[1024,128]{1,0:T(8,128)(2,1)S(1)} %copy-done.41, bf16[1024,128]{1,0:T(8,128)(2,1)S(1)} %copy-done.44, bf16[1024,128]{1,0:T(8,128)(2,1)} %collective-permute-done.2.refs_2_, bf16[1024,128]{1,0:T(8,128)(2,1)} %collective-permute-done.3.refs_3_, ...), custom_call_target="tpu_custom_call" | custom-call | flops 671088640 | bytes 4980736 | tf_op jit(solution)/shard_map/weight_grad/pallas_call | solution.py:287
  228.5 4.9 %weight_update.1 = (f32[512,1280]{1,0:T(8,128)}, f32[512,1280]{1,0:T(8,128)}, f32[512,1280]{1,0:T(8,128)}) custom-call(f32[512,1280]{1,0:T(8,128)S(1)} %weight_grad.5.grad_ref, bf16[512,1280]{1,0:T(8,128)(2,1)} %collective-permute-done.34.refs_0_, f32[512,1280]{1,0:T(8,128)S(1)} %copy-done, f32[512,1280]{1,0:T(8,128)S(1)} %copy-done.1, f32[512,1280]{1,0:T(8,128)S(1)} %copy-done.2), custom_call_target="tpu_custom_call" | custom-call | flops 13107200 | bytes 18350080 | tf_op jit(solution)/shard_map/weight_update/pallas_call | solution.py:334
  (170 shorter events, 62.4 us)
Async XLA Ops:
  17.6 10.6 %collective-permute-start.7 = (bf16[512,256]{1,0:T(8,128)(2,1)S(1)}, bf16[512,256]{1,0:T(8,128)(2,1)S(1)}, u32[]{:S(2)}, u32[]{:S(2)}) collective-permute-start(bf16[512,256]{1,0:T(8,128)(2,1)S(1)} %pad_maximum_fusion.1.refs_0_), channel_id=1, source_target_pairs={{0,2},{1,3},{2,0},{3,1},{4,6},{5,7},{6,4},{7,5},{8,10},{9,11},{10,... | collective-permute-start | bytes 786440 | tf_op jit(solution)/shard_map/ppermute | solution.py:26
  19.1 9.1 %collective-permute-start.8 = (bf16[512,256]{1,0:T(8,128)(2,1)S(1)}, bf16[512,256]{1,0:T(8,128)(2,1)S(1)}, u32[]{:S(2)}, u32[]{:S(2)}) collective-permute-start(bf16[512,256]{1,0:T(8,128)(2,1)S(1)} %pad_maximum_fusion.1.refs_0_), channel_id=1, source_target_pairs={{0,3},{1,2},{2,1},{3,0},{4,7},{5,6},{6,5},{7,4},{8,11},{9,10},{10,... | collective-permute-start | bytes 786440 | tf_op jit(solution)/shard_map/ppermute | solution.py:26
  41.7 14.3 %collective-permute-start.9 = (bf16[128,1024]{1,0:T(8,128)(2,1)S(1)}, bf16[128,1024]{1,0:T(8,128)(2,1)S(1)}, u32[]{:S(2)}, u32[]{:S(2)}) collective-permute-start(bf16[128,1024]{1,0:T(8,128)(2,1)S(1)} %get-tuple-element.28), channel_id=1, source_target_pairs={{0,8},{1,9},{2,10},{3,11},{4,12},{5,13},{6,14},{7,15},{8,0},{9,1},... | collective-permute-start | bytes 786440 | tf_op jit(solution)/shard_map/ppermute | solution.py:26
  56.1 18.9 %collective-permute-start.10 = (bf16[256,1024]{1,0:T(8,128)(2,1)S(1)}, bf16[256,1024]{1,0:T(8,128)(2,1)S(1)}, u32[]{:S(2)}, u32[]{:S(2)}) collective-permute-start(bf16[256,1024]{1,0:T(8,128)(2,1)S(1)} %pad_maximum_fusion), channel_id=1, source_target_pairs={{0,4},{1,5},{2,6},{3,7},{4,0},{5,1},{6,2},{7,3},{8,12},{9,13},{10,... | collective-permute-start | bytes 1572872 | tf_op jit(solution)/shard_map/ppermute | solution.py:26
  59.0 23.7 %collective-permute-start.21 = (bf16[1024,128]{1,0:T(8,128)(2,1)S(1)}, bf16[1024,128]{1,0:T(8,128)(2,1)S(1)}, u32[]{:S(2)}, u32[]{:S(2)}) collective-permute-start(bf16[1024,128]{1,0:T(8,128)(2,1)S(1)} %get-tuple-element.34), channel_id=1, source_target_pairs={{0,8},{1,9},{2,10},{3,11},{4,12},{5,13},{6,14},{7,15},{8,0},{9,1},... | collective-permute-start | bytes 786440 | tf_op jit(solution)/shard_map/ppermute | solution.py:26
  62.4 12.7 %collective-permute-start.15 = (bf16[512,256]{1,0:T(8,128)(2,1)S(1)}, bf16[512,256]{1,0:T(8,128)(2,1)S(1)}, u32[]{:S(2)}, u32[]{:S(2)}) collective-permute-start(bf16[512,256]{1,0:T(8,128)(2,1)S(1)} %get-tuple-element.30), channel_id=1, source_target_pairs={{0,1},{1,0},{2,3},{3,2},{4,5},{5,4},{6,7},{7,6},{8,9},{9,8},{10,11... | collective-permute-start | bytes 786440 | tf_op jit(solution)/shard_map/ppermute | solution.py:26
  63.8 14.9 %collective-permute-start.16 = (bf16[512,256]{1,0:T(8,128)(2,1)S(1)}, bf16[512,256]{1,0:T(8,128)(2,1)S(1)}, u32[]{:S(2)}, u32[]{:S(2)}) collective-permute-start(bf16[512,256]{1,0:T(8,128)(2,1)S(1)} %get-tuple-element.31), channel_id=1, source_target_pairs={{0,2},{1,3},{2,0},{3,1},{4,6},{5,7},{6,4},{7,5},{8,10},{9,11},{10,... | collective-permute-start | bytes 786440 | tf_op jit(solution)/shard_map/ppermute | solution.py:26
  64.4 15.8 %collective-permute-start.17 = (bf16[512,256]{1,0:T(8,128)(2,1)S(1)}, bf16[512,256]{1,0:T(8,128)(2,1)S(1)}, u32[]{:S(2)}, u32[]{:S(2)}) collective-permute-start(bf16[512,256]{1,0:T(8,128)(2,1)S(1)} %get-tuple-element.32), channel_id=1, source_target_pairs={{0,3},{1,2},{2,1},{3,0},{4,7},{5,6},{6,5},{7,4},{8,11},{9,10},{10,... | collective-permute-start | bytes 786440 | tf_op jit(solution)/shard_map/ppermute | solution.py:26
  75.0 8.3 %collective-permute-start.22 = (bf16[1024,128]{1,0:T(8,128)(2,1)S(1)}, bf16[1024,128]{1,0:T(8,128)(2,1)S(1)}, u32[]{:S(2)}, u32[]{:S(2)}) collective-permute-start(bf16[1024,128]{1,0:T(8,128)(2,1)S(1)} %get-tuple-element.35), channel_id=1, source_target_pairs={{0,4},{1,5},{2,6},{3,7},{4,0},{5,1},{6,2},{7,3},{8,12},{9,13},{10,... | collective-permute-start | bytes 786440 | tf_op jit(solution)/shard_map/ppermute | solution.py:26
  75.1 16.6 %collective-permute-start.23 = (bf16[1024,128]{1,0:T(8,128)(2,1)S(1)}, bf16[1024,128]{1,0:T(8,128)(2,1)S(1)}, u32[]{:S(2)}, u32[]{:S(2)}) collective-permute-start(bf16[1024,128]{1,0:T(8,128)(2,1)S(1)} %get-tuple-element.36), channel_id=1, source_target_pairs={{0,12},{1,13},{2,14},{3,15},{4,8},{5,9},{6,10},{7,11},{8,4},{9,5},... | collective-permute-start | bytes 786440 | tf_op jit(solution)/shard_map/ppermute | solution.py:26
  78.7 72.0 %collective-permute-start.11 = (bf16[512,1024]{1,0:T(8,128)(2,1)S(1)}, bf16[512,1024]{1,0:T(8,128)(2,1)S(1)}, u32[]{:S(2)}, u32[]{:S(2)}) collective-permute-start(bf16[512,1024]{1,0:T(8,128)(2,1)S(1)} %constant_dynamic-update-slice_fusion.refs_12_), channel_id=1, source_target_pairs={{0,1},{1,0},{2,3},{3,2},{4,5},{5,4},{6,7},{7,6},{8,9},{9,8},{10,11... | collective-permute-start | bytes 3145736 | tf_op jit(solution)/shard_map/ppermute | solution.py:26
  80.3 28.7 %collective-permute-start.18 = (bf16[512,256]{1,0:T(8,128)(2,1)S(1)}, bf16[512,256]{1,0:T(8,128)(2,1)S(1)}, u32[]{:S(2)}, u32[]{:S(2)}) collective-permute-start(bf16[512,256]{1,0:T(8,128)(2,1)S(1)} %fusion.1), channel_id=1, source_target_pairs={{0,8},{1,9},{2,10},{3,11},{4,12},{5,13},{6,14},{7,15},{8,0},{9,1},... | collective-permute-start | bytes 786440 | tf_op jit(solution)/shard_map/ppermute | solution.py:26
  82.7 39.3 %collective-permute-start.24 = (bf16[1024,128]{1,0:T(8,128)(2,1)S(1)}, bf16[1024,128]{1,0:T(8,128)(2,1)S(1)}, u32[]{:S(2)}, u32[]{:S(2)}) collective-permute-start(bf16[1024,128]{1,0:T(8,128)(2,1)S(1)} %get-tuple-element.37), channel_id=1, source_target_pairs={{0,1},{1,0},{2,3},{3,2},{4,5},{5,4},{6,7},{7,6},{8,9},{9,8},{10,11... | collective-permute-start | bytes 786440 | tf_op jit(solution)/shard_map/ppermute | solution.py:26
  83.4 39.4 %collective-permute-start.25 = (bf16[1024,128]{1,0:T(8,128)(2,1)S(1)}, bf16[1024,128]{1,0:T(8,128)(2,1)S(1)}, u32[]{:S(2)}, u32[]{:S(2)}) collective-permute-start(bf16[1024,128]{1,0:T(8,128)(2,1)S(1)} %get-tuple-element.38), channel_id=1, source_target_pairs={{0,9},{1,8},{2,11},{3,10},{4,13},{5,12},{6,15},{7,14},{8,1},{9,0},... | collective-permute-start | bytes 786440 | tf_op jit(solution)/shard_map/ppermute | solution.py:26
  92.4 31.2 %collective-permute-start.26 = (bf16[1024,128]{1,0:T(8,128)(2,1)S(1)}, bf16[1024,128]{1,0:T(8,128)(2,1)S(1)}, u32[]{:S(2)}, u32[]{:S(2)}) collective-permute-start(bf16[1024,128]{1,0:T(8,128)(2,1)S(1)} %get-tuple-element.39), channel_id=1, source_target_pairs={{0,5},{1,4},{2,7},{3,6},{4,1},{5,0},{6,3},{7,2},{8,13},{9,12},{10,... | collective-permute-start | bytes 786440 | tf_op jit(solution)/shard_map/ppermute | solution.py:26
  109.0 47.4 %collective-permute-start.13 = (bf16[512,1024]{1,0:T(8,128)(2,1)S(1)}, bf16[512,1024]{1,0:T(8,128)(2,1)S(1)}, u32[]{:S(2)}, u32[]{:S(2)}) collective-permute-start(bf16[512,1024]{1,0:T(8,128)(2,1)S(1)} %constant_dynamic-update-slice_fusion.refs_12_), channel_id=1, source_target_pairs={{0,2},{1,3},{2,0},{3,1},{4,6},{5,7},{6,4},{7,5},{8,10},{9,11},{10,... | collective-permute-start | bytes 3145736 | tf_op jit(solution)/shard_map/ppermute | solution.py:26
  122.7 9.3 %collective-permute-start.27 = (bf16[1024,128]{1,0:T(8,128)(2,1)S(1)}, bf16[1024,128]{1,0:T(8,128)(2,1)S(1)}, u32[]{:S(2)}, u32[]{:S(2)}) collective-permute-start(bf16[1024,128]{1,0:T(8,128)(2,1)S(1)} %get-tuple-element.40), channel_id=1, source_target_pairs={{0,13},{1,12},{2,15},{3,14},{4,9},{5,8},{6,11},{7,10},{8,5},{9,4},... | collective-permute-start | bytes 786440 | tf_op jit(solution)/shard_map/ppermute | solution.py:26
  123.4 16.8 %collective-permute-start.28 = (bf16[1024,128]{1,0:T(8,128)(2,1)S(1)}, bf16[1024,128]{1,0:T(8,128)(2,1)S(1)}, u32[]{:S(2)}, u32[]{:S(2)}) collective-permute-start(bf16[1024,128]{1,0:T(8,128)(2,1)S(1)} %get-tuple-element.41), channel_id=1, source_target_pairs={{0,2},{1,3},{2,0},{3,1},{4,6},{5,7},{6,4},{7,5},{8,10},{9,11},{10,... | collective-permute-start | bytes 786440 | tf_op jit(solution)/shard_map/ppermute | solution.py:26
  123.6 23.0 %collective-permute-start.19 = (bf16[512,256]{1,0:T(8,128)(2,1)S(1)}, bf16[512,256]{1,0:T(8,128)(2,1)S(1)}, u32[]{:S(2)}, u32[]{:S(2)}) collective-permute-start(bf16[512,256]{1,0:T(8,128)(2,1)S(1)} %fusion), channel_id=1, source_target_pairs={{0,4},{1,5},{2,6},{3,7},{4,0},{5,1},{6,2},{7,3},{8,12},{9,13},{10,... | collective-permute-start | bytes 786440 | tf_op jit(solution)/shard_map/ppermute | solution.py:26
  132.0 25.2 %collective-permute-start.29 = (bf16[1024,128]{1,0:T(8,128)(2,1)S(1)}, bf16[1024,128]{1,0:T(8,128)(2,1)S(1)}, u32[]{:S(2)}, u32[]{:S(2)}) collective-permute-start(bf16[1024,128]{1,0:T(8,128)(2,1)S(1)} %get-tuple-element.42), channel_id=1, source_target_pairs={{0,10},{1,11},{2,8},{3,9},{4,14},{5,15},{6,12},{7,13},{8,2},{9,3},... | collective-permute-start | bytes 786440 | tf_op jit(solution)/shard_map/ppermute | solution.py:26
  140.3 18.9 %collective-permute-start.30 = (bf16[1024,128]{1,0:T(8,128)(2,1)S(1)}, bf16[1024,128]{1,0:T(8,128)(2,1)S(1)}, u32[]{:S(2)}, u32[]{:S(2)}) collective-permute-start(bf16[1024,128]{1,0:T(8,128)(2,1)S(1)} %get-tuple-element.43), channel_id=1, source_target_pairs={{0,6},{1,7},{2,4},{3,5},{4,2},{5,3},{6,0},{7,1},{8,14},{9,15},{10,... | collective-permute-start | bytes 786440 | tf_op jit(solution)/shard_map/ppermute | solution.py:26
  146.6 15.5 %collective-permute-start.31 = (bf16[1024,128]{1,0:T(8,128)(2,1)S(1)}, bf16[1024,128]{1,0:T(8,128)(2,1)S(1)}, u32[]{:S(2)}, u32[]{:S(2)}) collective-permute-start(bf16[1024,128]{1,0:T(8,128)(2,1)S(1)} %get-tuple-element.44), channel_id=1, source_target_pairs={{0,14},{1,15},{2,12},{3,13},{4,10},{5,11},{6,8},{7,9},{8,6},{9,7},... | collective-permute-start | bytes 786440 | tf_op jit(solution)/shard_map/ppermute | solution.py:26
  150.7 14.4 %collective-permute-start = (bf16[1024,128]{1,0:T(8,128)(2,1)S(1)}, bf16[1024,128]{1,0:T(8,128)(2,1)S(1)}, u32[]{:S(2)}, u32[]{:S(2)}) collective-permute-start(bf16[1024,128]{1,0:T(8,128)(2,1)S(1)} %get-tuple-element.24), channel_id=1, source_target_pairs={{0,3},{1,2},{2,1},{3,0},{4,7},{5,6},{6,5},{7,4},{8,11},{9,10},{10,... | collective-permute-start | bytes 786440 | tf_op jit(solution)/shard_map/ppermute | solution.py:26
  156.4 13.5 %collective-permute-start.1 = (bf16[1024,128]{1,0:T(8,128)(2,1)S(1)}, bf16[1024,128]{1,0:T(8,128)(2,1)S(1)}, u32[]{:S(2)}, u32[]{:S(2)}) collective-permute-start(bf16[1024,128]{1,0:T(8,128)(2,1)S(1)} %get-tuple-element.25), channel_id=1, source_target_pairs={{0,11},{1,10},{2,9},{3,8},{4,15},{5,14},{6,13},{7,12},{8,3},{9,2},... | collective-permute-start | bytes 786440 | tf_op jit(solution)/shard_map/ppermute | solution.py:26
  157.9 22.8 %collective-permute-start.32 = (bf16[512,256]{1,0:T(8,128)(2,1)S(1)}, bf16[512,256]{1,0:T(8,128)(2,1)S(1)}, u32[]{:S(2)}, u32[]{:S(2)}) collective-permute-start(bf16[512,256]{1,0:T(8,128)(2,1)S(1)} %add_convert_fusion.refs_15_), channel_id=1, source_target_pairs={{0,1},{1,0},{2,3},{3,2},{4,5},{5,4},{6,7},{7,6},{8,9},{9,8},{10,11... | collective-permute-start | bytes 786440 | tf_op jit(solution)/shard_map/ppermute | solution.py:26
  159.8 21.6 %collective-permute-start.33 = (bf16[512,256]{1,0:T(8,128)(2,1)S(1)}, bf16[512,256]{1,0:T(8,128)(2,1)S(1)}, u32[]{:S(2)}, u32[]{:S(2)}) collective-permute-start(bf16[512,256]{1,0:T(8,128)(2,1)S(1)} %add_convert_fusion.refs_15_), channel_id=1, source_target_pairs={{0,2},{1,3},{2,0},{3,1},{4,6},{5,7},{6,4},{7,5},{8,10},{9,11},{10,... | collective-permute-start | bytes 786440 | tf_op jit(solution)/shard_map/ppermute | solution.py:26
  162.8 43.6 %collective-permute-start.12 = (bf16[512,512]{1,0:T(8,128)(2,1)}, bf16[512,512]{1,0:T(8,128)(2,1)}, u32[]{:S(2)}, u32[]{:S(2)}) collective-permute-start(bf16[512,512]{1,0:T(8,128)(2,1)} %slice.44), channel_id=1, source_target_pairs={{0,2},{1,3},{2,0},{3,1},{4,6},{5,7},{6,4},{7,5},{8,10},{9,11},{10,... | collective-permute-start | bytes 1572872 | tf_op jit(solution)/shard_map/ppermute | solution.py:26
  165.8 40.6 %collective-permute-start.14 = (bf16[512,512]{1,0:T(8,128)(2,1)}, bf16[512,512]{1,0:T(8,128)(2,1)}, u32[]{:S(2)}, u32[]{:S(2)}) collective-permute-start(bf16[512,512]{1,0:T(8,128)(2,1)} %slice.45), channel_id=1, source_target_pairs={{0,1},{1,0},{2,3},{3,2},{4,5},{5,4},{6,7},{7,6},{8,9},{9,8},{10,11... | collective-permute-start | bytes 1572872 | tf_op jit(solution)/shard_map/ppermute | solution.py:26
  170.6 35.8 %collective-permute-start.2 = (bf16[1024,128]{1,0:T(8,128)(2,1)}, bf16[1024,128]{1,0:T(8,128)(2,1)}, u32[]{:S(2)}, u32[]{:S(2)}) collective-permute-start(bf16[1024,128]{1,0:T(8,128)(2,1)} %get-tuple-element.26), channel_id=1, source_target_pairs={{0,7},{1,6},{2,5},{3,4},{4,3},{5,2},{6,1},{7,0},{8,15},{9,14},{10,... | collective-permute-start | bytes 786440 | tf_op jit(solution)/shard_map/ppermute | solution.py:26
  181.5 24.9 %collective-permute-start.3 = (bf16[1024,128]{1,0:T(8,128)(2,1)}, bf16[1024,128]{1,0:T(8,128)(2,1)}, u32[]{:S(2)}, u32[]{:S(2)}) collective-permute-start(bf16[1024,128]{1,0:T(8,128)(2,1)} %get-tuple-element.27), channel_id=1, source_target_pairs={{0,15},{1,14},{2,13},{3,12},{4,11},{5,10},{6,9},{7,8},{8,7},{9,6},... | collective-permute-start | bytes 786440 | tf_op jit(solution)/shard_map/ppermute | solution.py:26
  182.2 24.2 %collective-permute-start.20 = (bf16[512,256]{1,0:T(8,128)(2,1)S(1)}, bf16[512,256]{1,0:T(8,128)(2,1)}, u32[]{:S(2)}, u32[]{:S(2)}) collective-permute-start(bf16[512,256]{1,0:T(8,128)(2,1)S(1)} %add_convert_fusion.refs_15_), channel_id=1, source_target_pairs={{0,3},{1,2},{2,1},{3,0},{4,7},{5,6},{6,5},{7,4},{8,11},{9,10},{10,... | collective-permute-start | bytes 786440 | tf_op jit(solution)/shard_map/ppermute | solution.py:26
  209.8 18.1 %collective-permute-start.34 = (bf16[512,1280]{1,0:T(8,128)(2,1)}, bf16[512,1280]{1,0:T(8,128)(2,1)}, u32[]{:S(2)}, u32[]{:S(2)}) collective-permute-start(bf16[512,1280]{1,0:T(8,128)(2,1)} %weight_grad.7), channel_id=1, source_target_pairs={{0,16},{16,0},{1,17},{17,1},{2,18},{18,2},{3,19},{19,3},{4,20},{20... | collective-permute-start | bytes 3932168 | tf_op jit(solution)/shard_map/ppermute | solution.py:390
  (57 other events, 192.5 us)

commit v2 on v1

--- a/solution.py
+++ b/solution.py
@@ -363,15 +363,13 @@
     me = lax.axis_index("ctx").astype(jnp.int32).reshape(1)
     dp_rank = lax.axis_index("dp").astype(jnp.int32)
 
-    x_groups = []
+    blocks = {}
     for j in range(4):
-        masks = tuple(o ^ j for o in order)
+        masks = tuple(o ^ j for o in order if o ^ j) + (0,) * (j == 3)
         packed = pack(layer_input[0], me, masks, dp_count, ctx_count, own_rows)
-        blocks = []
-        for i, o in enumerate(order):
-            block = packed[i]
-            blocks.append(block if o ^ j == 0 else swap(block, o ^ j, ctx_count))
-        x_groups.append(blocks)
+        for mask, block in zip(masks, packed):
+            blocks[mask] = swap(block, mask, ctx_count) if mask else block
+    x_groups = [[blocks[o ^ j] for o in order] for j in range(4)]
 
     kv_parts = spread(jnp.concatenate([key_rows[0], value_rows[0]], axis=1), ctx_count)
     dq, dkv_terms = attention(me, block_order, query_rows[0], out_grad[0], kv_parts, order)

time: 235 us -> 232 us (0.987)
  starting transfers between devices: 84.3 us -> 76.9 us
  waiting for transfers between devices: 72.3 us -> 75.6 us
    ppermute x34, starting transfers between devices: 84.3 us -> 76.9 us  [swap(): return lax.ppermute(block, 'ctx', [(i, i ^ mask) for i in range(count)])]
    ppermute x34, waiting for transfers between devices: 72.3 us -> 75.6 us  [swap(): return lax.ppermute(block, 'ctx', [(i, i ^ mask) for i in range(count)])]
  transfers between devices with their start and end apart: 35 -> 35, of which waited for: 12 -> 15; matrix products, arithmetic and copies ran while one was open for 1% -> 1% of each run, Pallas kernels for 6% -> 6%
where the time goes in v2:
time: 232 us; the launch traced here: 230 us
  starting transfers between devices  76.9 us (33%)
  waiting for transfers between devices  75.6 us (33%)
  local copies, waits for them, and re-layouts  40 us (17%)
  Pallas kernels  33.8 us (15%)
  other arithmetic  2.93 us (1%)
    ppermute x34, starting transfers between devices, swap(): return lax.ppermute(block, 'ctx', [(i, i ^ mask) for i in range(count)])  76.9 us
    ppermute x34, waiting for transfers between devices, swap(): return lax.ppermute(block, 'ctx', [(i, i ^ mask) for i in range(count)])  75.6 us
    unnamed x110, local copies, waits for them, and re-layouts  38.3 us
    pallas_call x1, Pallas kernels, attention(): pl.pallas_call(functools.partial(attention_kernel, order), grid_spec=pltp...  11 us
    pallas_call x4, Pallas kernels, grad_call(): pl.pallas_call(functools.partial(grad_kernel, [len(halves) for halves in...  10.3 us
    pallas_call x4, Pallas kernels, pack(): pl.pallas_call(functools.partial(pack_kernel, masks, dp_count, ctx_count)...  7.64 us
    pallas_call x1, Pallas kernels, update_call(): pl.pallas_call(functools.partial(update_kernel, len(others), tile), in_sp...  4.9 us
  transfers between devices with their start and end apart: 35, of which 15 were waited for; matrix products, arithmetic and copies ran while one was open for 1% of the time, Pallas kernels for 6%

profile of v2, /device:TPU:0, one launch (start us, length us, event | category | flops | bytes accessed | tf_op | source)
XLA Modules:
  0.0 230.4 jit_solution(1530894151881274857)
XLA Ops:
  1.4 4.1 %collective-permute-start.4 = (bf16[128,256]{1,0:T(8,128)(2,1)S(1)}, bf16[128,256]{1,0:T(8,128)(2,1)S(1)}, u32[]{:S(2)}, u32[]{:S(2)}) collective-permute-start(bf16[128,256]{1,0:T(8,128)(2,1)S(1)} %pad_maximum_fusion.4), channel_id=1, source_target_pairs={{0,8},{1,9},{2,10},{3,11},{4,12},{5,13},{6,14},{7,15},{8,0},{9,1},... | collective-permute-start | bytes 196616 | tf_op jit(solution)/shard_map/ppermute | solution.py:26
  5.5 3.6 %collective-permute-done.4 = bf16[128,256]{1,0:T(8,128)(2,1)S(1)} collective-permute-done((bf16[128,256]{1,0:T(8,128)(2,1)S(1)}, bf16[128,256]{1,0:T(8,128)(2,1)S(1)}, u32[]{:S(2)}, u32[]{:S(2)}) %collective-permute-start.4) | collective-permute-done | bytes 65568 | tf_op jit(solution)/shard_map/ppermute | solution.py:26
  10.6 4.4 %collective-permute-done.5 = bf16[256,256]{1,0:T(8,128)(2,1)S(1)} collective-permute-done((bf16[256,256]{1,0:T(8,128)(2,1)S(1)}, bf16[256,256]{1,0:T(8,128)(2,1)S(1)}, u32[]{:S(2)}, u32[]{:S(2)}) %collective-permute-start.5) | collective-permute-done | bytes 131104 | tf_op jit(solution)/shard_map/ppermute | solution.py:26
  15.8 1.8 collective-permute-start.6
  19.4 4.8 %collective-permute-done.6.refs_1_ = bf16[512,256]{1,0:T(8,128)(2,1)S(1)} collective-permute-done((bf16[512,256]{1,0:T(8,128)(2,1)S(1)}, bf16[512,256]{1,0:T(8,128)(2,1)S(1)}, u32[]{:S(2)}, u32[]{:S(2)}) %collective-permute-start.6) | collective-permute-done | bytes 262176 | tf_op jit(solution)/shard_map/ppermute | solution.py:26
  24.1 4.1 %collective-permute-done.7.refs_2_ = bf16[512,256]{1,0:T(8,128)(2,1)S(1)} collective-permute-done((bf16[512,256]{1,0:T(8,128)(2,1)S(1)}, bf16[512,256]{1,0:T(8,128)(2,1)S(1)}, u32[]{:S(2)}, u32[]{:S(2)}) %collective-permute-start.7) | collective-permute-done | bytes 262176 | tf_op jit(solution)/shard_map/ppermute | solution.py:26
  30.8 11.0 %attention.1 = (bf16[128,1024]{1,0:T(8,128)(2,1)S(1)}, bf16[512,256]{1,0:T(8,128)(2,1)S(1)}, bf16[512,256]{1,0:T(8,128)(2,1)S(1)}, bf16[512,256]{1,0:T(8,128)(2,1)S(1)}, bf16[512,256]{1,0:T(8,128)(2,1)S(1)}) custom-call(s32[1]{0:T(128)} %bitcast.1.me_ref, s32[32]{0:T(128)S(1)} %copy-done.53, bf16[128,1024]{1,0:T(8,128)(2,1)S(1)} %bitcast.8, ...), custom_call_target="tpu_custom_call" | custom-call | flops 2684354560 | bytes 2097152 | tf_op jit(solution)/shard_map/attention/pallas_call | solution.py:209
  41.7 4.2 %collective-permute-start.9 = (bf16[128,1024]{1,0:T(8,128)(2,1)S(1)}, bf16[128,1024]{1,0:T(8,128)(2,1)S(1)}, u32[]{:S(2)}, u32[]{:S(2)}) collective-permute-start(bf16[128,1024]{1,0:T(8,128)(2,1)S(1)} %get-tuple-element.28), channel_id=1, source_target_pairs={{0,8},{1,9},{2,10},{3,11},{4,12},{5,13},{6,14},{7,15},{8,0},{9,1},... | collective-permute-start | bytes 786440 | tf_op jit(solution)/shard_map/ppermute | solution.py:26
  45.9 10.1 %collective-permute-done.9 = bf16[128,1024]{1,0:T(8,128)(2,1)S(1)} collective-permute-done((bf16[128,1024]{1,0:T(8,128)(2,1)S(1)}, bf16[128,1024]{1,0:T(8,128)(2,1)S(1)}, u32[]{:S(2)}, u32[]{:S(2)}) %collective-permute-start.9) | collective-permute-done | bytes 262176 | tf_op jit(solution)/shard_map/ppermute | solution.py:26
  60.9 2.4 %collective-permute-start.17 = (bf16[512,256]{1,0:T(8,128)(2,1)S(1)}, bf16[512,256]{1,0:T(8,128)(2,1)S(1)}, u32[]{:S(2)}, u32[]{:S(2)}) collective-permute-start(bf16[512,256]{1,0:T(8,128)(2,1)S(1)} %get-tuple-element.32), channel_id=1, source_target_pairs={{0,3},{1,2},{2,1},{3,0},{4,7},{5,6},{6,5},{7,4},{8,11},{9,10},{10,... | collective-permute-start | bytes 786440 | tf_op jit(solution)/shard_map/ppermute | solution.py:26
  63.4 6.0 %collective-permute-done.10 = bf16[256,1024]{1,0:T(8,128)(2,1)S(1)} collective-permute-done((bf16[256,1024]{1,0:T(8,128)(2,1)S(1)}, bf16[256,1024]{1,0:T(8,128)(2,1)S(1)}, u32[]{:S(2)}, u32[]{:S(2)}) %collective-permute-start.10) | collective-permute-done | bytes 524320 | tf_op jit(solution)/shard_map/ppermute | solution.py:26
  69.4 3.3 %collective-permute-start.25 = (bf16[1024,128]{1,0:T(8,128)(2,1)S(1)}, bf16[1024,128]{1,0:T(8,128)(2,1)S(1)}, u32[]{:S(2)}, u32[]{:S(2)}) collective-permute-start(bf16[1024,128]{1,0:T(8,128)(2,1)S(1)} %get-tuple-element.38), channel_id=1, source_target_pairs={{0,9},{1,8},{2,11},{3,10},{4,13},{5,12},{6,15},{7,14},{8,1},{9,0},... | collective-permute-start | bytes 786440 | tf_op jit(solution)/shard_map/ppermute | solution.py:26
  74.2 9.9 %collective-permute-start.26 = (bf16[1024,128]{1,0:T(8,128)(2,1)S(1)}, bf16[1024,128]{1,0:T(8,128)(2,1)S(1)}, u32[]{:S(2)}, u32[]{:S(2)}) collective-permute-start(bf16[1024,128]{1,0:T(8,128)(2,1)S(1)} %get-tuple-element.39), channel_id=1, source_target_pairs={{0,5},{1,4},{2,7},{3,6},{4,1},{5,0},{6,3},{7,2},{8,13},{9,12},{10,... | collective-permute-start | bytes 786440 | tf_op jit(solution)/shard_map/ppermute | solution.py:26
  84.6 5.3 %collective-permute-done.17 = bf16[512,256]{1,0:T(8,128)(2,1)S(1)} collective-permute-done((bf16[512,256]{1,0:T(8,128)(2,1)S(1)}, bf16[512,256]{1,0:T(8,128)(2,1)S(1)}, u32[]{:S(2)}, u32[]{:S(2)}) %collective-permute-start.17) | collective-permute-done | bytes 262176 | tf_op jit(solution)/shard_map/ppermute | solution.py:26
  90.1 3.4 %collective-permute-start.18 = (bf16[512,256]{1,0:T(8,128)(2,1)S(1)}, bf16[512,256]{1,0:T(8,128)(2,1)S(1)}, u32[]{:S(2)}, u32[]{:S(2)}) collective-permute-start(bf16[512,256]{1,0:T(8,128)(2,1)S(1)} %fusion.1), channel_id=1, source_target_pairs={{0,8},{1,9},{2,10},{3,11},{4,12},{5,13},{6,14},{7,15},{8,0},{9,1},... | collective-permute-start | bytes 786440 | tf_op jit(solution)/shard_map/ppermute | solution.py:26
  101.3 13.4 %collective-permute-done.18 = bf16[512,256]{1,0:T(8,128)(2,1)S(1)} collective-permute-done((bf16[512,256]{1,0:T(8,128)(2,1)S(1)}, bf16[512,256]{1,0:T(8,128)(2,1)S(1)}, u32[]{:S(2)}, u32[]{:S(2)}) %collective-permute-start.18) | collective-permute-done | bytes 262176 | tf_op jit(solution)/shard_map/ppermute | solution.py:26
  116.5 6.3 %collective-permute-start.30 = (bf16[1024,128]{1,0:T(8,128)(2,1)S(1)}, bf16[1024,128]{1,0:T(8,128)(2,1)S(1)}, u32[]{:S(2)}, u32[]{:S(2)}) collective-permute-start(bf16[1024,128]{1,0:T(8,128)(2,1)S(1)} %get-tuple-element.43), channel_id=1, source_target_pairs={{0,6},{1,7},{2,4},{3,5},{4,2},{5,3},{6,0},{7,1},{8,14},{9,15},{10,... | collective-permute-start | bytes 786440 | tf_op jit(solution)/shard_map/ppermute | solution.py:26
  124.8 2.7 %pack_rows.4 = (bf16[1024,128]{1,0:T(8,128)(2,1)S(1)}, bf16[1024,128]{1,0:T(8,128)(2,1)S(1)}, bf16[1024,128]{1,0:T(8,128)(2,1)}, bf16[1024,128]{1,0:T(8,128)(2,1)}, bf16[1024,128]{1,0:T(8,128)(2,1)S(1)}) custom-call(s32[1]{0:T(128)} %bitcast.1.me_ref, bf16[128,16384]{1,0:T(8,128)(2,1)} %bitcast.12), custom_call_target="tpu_custom_call" | custom-call | bytes 2621440 | tf_op jit(solution)/shard_map/pack_rows/pallas_call | solution.py:106
  129.1 3.9 %collective-permute-done.30.refs_10_ = bf16[1024,128]{1,0:T(8,128)(2,1)S(1)} collective-permute-done((bf16[1024,128]{1,0:T(8,128)(2,1)S(1)}, bf16[1024,128]{1,0:T(8,128)(2,1)S(1)}, u32[]{:S(2)}, u32[]{:S(2)}) %collective-permute-start.30) | collective-permute-done | bytes 262176 | tf_op jit(solution)/shard_map/ppermute | solution.py:26
  133.1 3.5 %collective-permute-done.31.refs_11_ = bf16[1024,128]{1,0:T(8,128)(2,1)S(1)} collective-permute-done((bf16[1024,128]{1,0:T(8,128)(2,1)S(1)}, bf16[1024,128]{1,0:T(8,128)(2,1)S(1)}, u32[]{:S(2)}, u32[]{:S(2)}) %collective-permute-start.31) | collective-permute-done | bytes 262176 | tf_op jit(solution)/shard_map/ppermute | solution.py:26
  137.1 7.5 %collective-permute-done.19 = bf16[512,256]{1,0:T(8,128)(2,1)S(1)} collective-permute-done((bf16[512,256]{1,0:T(8,128)(2,1)S(1)}, bf16[512,256]{1,0:T(8,128)(2,1)S(1)}, u32[]{:S(2)}, u32[]{:S(2)}) %collective-permute-start.19) | collective-permute-done | bytes 262176 | tf_op jit(solution)/shard_map/ppermute | solution.py:26
  144.6 2.3 %collective-permute-start.23 = (bf16[1024,128]{1,0:T(8,128)(2,1)S(1)}, bf16[1024,128]{1,0:T(8,128)(2,1)S(1)}, u32[]{:S(2)}, u32[]{:S(2)}) collective-permute-start(bf16[1024,128]{1,0:T(8,128)(2,1)S(1)} %get-tuple-element.36), channel_id=1, source_target_pairs={{0,12},{1,13},{2,14},{3,15},{4,8},{5,9},{6,10},{7,11},{8,4},{9,5},... | collective-permute-start | bytes 786440 | tf_op jit(solution)/shard_map/ppermute | solution.py:26
  146.9 3.0 %collective-permute-start = (bf16[1024,128]{1,0:T(8,128)(2,1)S(1)}, bf16[1024,128]{1,0:T(8,128)(2,1)S(1)}, u32[]{:S(2)}, u32[]{:S(2)}) collective-permute-start(bf16[1024,128]{1,0:T(8,128)(2,1)S(1)} %get-tuple-element.24), channel_id=1, source_target_pairs={{0,3},{1,2},{2,1},{3,0},{4,7},{5,6},{6,5},{7,4},{8,11},{9,10},{10,... | collective-permute-start | bytes 786440 | tf_op jit(solution)/shard_map/ppermute | solution.py:26
  152.6 7.2 %collective-permute-start.32 = (bf16[512,256]{1,0:T(8,128)(2,1)S(1)}, bf16[512,256]{1,0:T(8,128)(2,1)S(1)}, u32[]{:S(2)}, u32[]{:S(2)}) collective-permute-start(bf16[512,256]{1,0:T(8,128)(2,1)S(1)} %add_convert_fusion.refs_15_), channel_id=1, source_target_pairs={{0,1},{1,0},{2,3},{3,2},{4,5},{5,4},{6,7},{7,6},{8,9},{9,8},{10,11... | collective-permute-start | bytes 786440 | tf_op jit(solution)/shard_map/ppermute | solution.py:26
  161.2 2.0 collective-permute-start.12
  164.0 6.6 %collective-permute-done.1.refs_1_ = bf16[1024,128]{1,0:T(8,128)(2,1)S(1)} collective-permute-done((bf16[1024,128]{1,0:T(8,128)(2,1)S(1)}, bf16[1024,128]{1,0:T(8,128)(2,1)S(1)}, u32[]{:S(2)}, u32[]{:S(2)}) %collective-permute-start.1) | collective-permute-done | bytes 262176 | tf_op jit(solution)/shard_map/ppermute | solution.py:26
  172.2 14.7 %collective-permute-start.3 = (bf16[1024,128]{1,0:T(8,128)(2,1)}, bf16[1024,128]{1,0:T(8,128)(2,1)}, u32[]{:S(2)}, u32[]{:S(2)}) collective-permute-start(bf16[1024,128]{1,0:T(8,128)(2,1)} %get-tuple-element.27), channel_id=1, source_target_pairs={{0,15},{1,14},{2,13},{3,12},{4,11},{5,10},{6,9},{7,8},{8,7},{9,6},... | collective-permute-start | bytes 786440 | tf_op jit(solution)/shard_map/ppermute | solution.py:26
  201.0 2.2 weight_grad.6.refs_7_
  203.3 3.4 %weight_grad.7 = bf16[512,1280]{1,0:T(8,128)(2,1)} custom-call(s32[1]{0:T(128)} %bitcast.7.slab_ref, bf16[1024,128]{1,0:T(8,128)(2,1)S(1)} %copy-done.40, bf16[1024,128]{1,0:T(8,128)(2,1)S(1)} %copy-done.43, bf16[1024,128]{1,0:T(8,128)(2,1)} %collective-permute-done.2.refs_2_, bf16[1024,128]{1,0:T(8,128)(2,1)} %collective-permute-done.3.refs_3_, ...), custom_call_target="tpu_custom_call" | custom-call | flops 671088640 | bytes 4980736 | tf_op jit(solution)/shard_map/weight_grad/pallas_call | solution.py:287
  220.0 2.3 weight_grad.4.refs_7_
  222.3 2.5 %weight_grad.5.grad_ref = f32[512,1280]{1,0:T(8,128)S(1)} custom-call(s32[1]{0:T(128)} %bitcast.slab_ref, bf16[1024,128]{1,0:T(8,128)(2,1)S(1)} %copy-done.41, bf16[1024,128]{1,0:T(8,128)(2,1)S(1)} %copy-done.44, bf16[1024,128]{1,0:T(8,128)(2,1)} %collective-permute-done.2.refs_2_, bf16[1024,128]{1,0:T(8,128)(2,1)} %collective-permute-done.3.refs_3_, ...), custom_call_target="tpu_custom_call" | custom-call | flops 671088640 | bytes 4980736 | tf_op jit(solution)/shard_map/weight_grad/pallas_call | solution.py:287
  225.4 4.9 %weight_update.1 = (f32[512,1280]{1,0:T(8,128)}, f32[512,1280]{1,0:T(8,128)}, f32[512,1280]{1,0:T(8,128)}) custom-call(f32[512,1280]{1,0:T(8,128)S(1)} %weight_grad.5.grad_ref, bf16[512,1280]{1,0:T(8,128)(2,1)} %collective-permute-done.34.refs_0_, f32[512,1280]{1,0:T(8,128)S(1)} %copy-done, f32[512,1280]{1,0:T(8,128)S(1)} %copy-done.1, f32[512,1280]{1,0:T(8,128)S(1)} %copy-done.2), custom_call_target="tpu_custom_call" | custom-call | flops 13107200 | bytes 18350080 | tf_op jit(solution)/shard_map/weight_update/pallas_call | solution.py:334
  (170 shorter events, 62.4 us)
Async XLA Ops:
  17.6 10.6 %collective-permute-start.7 = (bf16[512,256]{1,0:T(8,128)(2,1)S(1)}, bf16[512,256]{1,0:T(8,128)(2,1)S(1)}, u32[]{:S(2)}, u32[]{:S(2)}) collective-permute-start(bf16[512,256]{1,0:T(8,128)(2,1)S(1)} %pad_maximum_fusion.1.refs_0_), channel_id=1, source_target_pairs={{0,2},{1,3},{2,0},{3,1},{4,6},{5,7},{6,4},{7,5},{8,10},{9,11},{10,... | collective-permute-start | bytes 786440 | tf_op jit(solution)/shard_map/ppermute | solution.py:26
  19.1 9.1 %collective-permute-start.8 = (bf16[512,256]{1,0:T(8,128)(2,1)S(1)}, bf16[512,256]{1,0:T(8,128)(2,1)S(1)}, u32[]{:S(2)}, u32[]{:S(2)}) collective-permute-start(bf16[512,256]{1,0:T(8,128)(2,1)S(1)} %pad_maximum_fusion.1.refs_0_), channel_id=1, source_target_pairs={{0,3},{1,2},{2,1},{3,0},{4,7},{5,6},{6,5},{7,4},{8,11},{9,10},{10,... | collective-permute-start | bytes 786440 | tf_op jit(solution)/shard_map/ppermute | solution.py:26
  41.7 14.3 %collective-permute-start.9 = (bf16[128,1024]{1,0:T(8,128)(2,1)S(1)}, bf16[128,1024]{1,0:T(8,128)(2,1)S(1)}, u32[]{:S(2)}, u32[]{:S(2)}) collective-permute-start(bf16[128,1024]{1,0:T(8,128)(2,1)S(1)} %get-tuple-element.28), channel_id=1, source_target_pairs={{0,8},{1,9},{2,10},{3,11},{4,12},{5,13},{6,14},{7,15},{8,0},{9,1},... | collective-permute-start | bytes 786440 | tf_op jit(solution)/shard_map/ppermute | solution.py:26
  56.1 13.3 %collective-permute-start.10 = (bf16[256,1024]{1,0:T(8,128)(2,1)S(1)}, bf16[256,1024]{1,0:T(8,128)(2,1)S(1)}, u32[]{:S(2)}, u32[]{:S(2)}) collective-permute-start(bf16[256,1024]{1,0:T(8,128)(2,1)S(1)} %pad_maximum_fusion), channel_id=1, source_target_pairs={{0,4},{1,5},{2,6},{3,7},{4,0},{5,1},{6,2},{7,3},{8,12},{9,13},{10,... | collective-permute-start | bytes 1572872 | tf_op jit(solution)/shard_map/ppermute | solution.py:26
  58.3 36.9 %collective-permute-start.24 = (bf16[1024,128]{1,0:T(8,128)(2,1)S(1)}, bf16[1024,128]{1,0:T(8,128)(2,1)S(1)}, u32[]{:S(2)}, u32[]{:S(2)}) collective-permute-start(bf16[1024,128]{1,0:T(8,128)(2,1)S(1)} %get-tuple-element.37), channel_id=1, source_target_pairs={{0,1},{1,0},{2,3},{3,2},{4,5},{5,4},{6,7},{7,6},{8,9},{9,8},{10,11... | collective-permute-start | bytes 786440 | tf_op jit(solution)/shard_map/ppermute | solution.py:26
  59.8 14.3 %collective-permute-start.15 = (bf16[512,256]{1,0:T(8,128)(2,1)S(1)}, bf16[512,256]{1,0:T(8,128)(2,1)S(1)}, u32[]{:S(2)}, u32[]{:S(2)}) collective-permute-start(bf16[512,256]{1,0:T(8,128)(2,1)S(1)} %get-tuple-element.30), channel_id=1, source_target_pairs={{0,1},{1,0},{2,3},{3,2},{4,5},{5,4},{6,7},{7,6},{8,9},{9,8},{10,11... | collective-permute-start | bytes 786440 | tf_op jit(solution)/shard_map/ppermute | solution.py:26
  60.4 23.7 %collective-permute-start.16 = (bf16[512,256]{1,0:T(8,128)(2,1)S(1)}, bf16[512,256]{1,0:T(8,128)(2,1)S(1)}, u32[]{:S(2)}, u32[]{:S(2)}) collective-permute-start(bf16[512,256]{1,0:T(8,128)(2,1)S(1)} %get-tuple-element.31), channel_id=1, source_target_pairs={{0,2},{1,3},{2,0},{3,1},{4,6},{5,7},{6,4},{7,5},{8,10},{9,11},{10,... | collective-permute-start | bytes 786440 | tf_op jit(solution)/shard_map/ppermute | solution.py:26
  60.9 29.1 %collective-permute-start.17 = (bf16[512,256]{1,0:T(8,128)(2,1)S(1)}, bf16[512,256]{1,0:T(8,128)(2,1)S(1)}, u32[]{:S(2)}, u32[]{:S(2)}) collective-permute-start(bf16[512,256]{1,0:T(8,128)(2,1)S(1)} %get-tuple-element.32), channel_id=1, source_target_pairs={{0,3},{1,2},{2,1},{3,0},{4,7},{5,6},{6,5},{7,4},{8,11},{9,10},{10,... | collective-permute-start | bytes 786440 | tf_op jit(solution)/shard_map/ppermute | solution.py:26
  69.4 28.1 %collective-permute-start.25 = (bf16[1024,128]{1,0:T(8,128)(2,1)S(1)}, bf16[1024,128]{1,0:T(8,128)(2,1)S(1)}, u32[]{:S(2)}, u32[]{:S(2)}) collective-permute-start(bf16[1024,128]{1,0:T(8,128)(2,1)S(1)} %get-tuple-element.38), channel_id=1, source_target_pairs={{0,9},{1,8},{2,11},{3,10},{4,13},{5,12},{6,15},{7,14},{8,1},{9,0},... | collective-permute-start | bytes 786440 | tf_op jit(solution)/shard_map/ppermute | solution.py:26
  74.2 25.5 %collective-permute-start.26 = (bf16[1024,128]{1,0:T(8,128)(2,1)S(1)}, bf16[1024,128]{1,0:T(8,128)(2,1)S(1)}, u32[]{:S(2)}, u32[]{:S(2)}) collective-permute-start(bf16[1024,128]{1,0:T(8,128)(2,1)S(1)} %get-tuple-element.39), channel_id=1, source_target_pairs={{0,5},{1,4},{2,7},{3,6},{4,1},{5,0},{6,3},{7,2},{8,13},{9,12},{10,... | collective-permute-start | bytes 786440 | tf_op jit(solution)/shard_map/ppermute | solution.py:26
  84.1 62.9 %collective-permute-start.11 = (bf16[512,1024]{1,0:T(8,128)(2,1)S(1)}, bf16[512,1024]{1,0:T(8,128)(2,1)S(1)}, u32[]{:S(2)}, u32[]{:S(2)}) collective-permute-start(bf16[512,1024]{1,0:T(8,128)(2,1)S(1)} %constant_dynamic-update-slice_fusion.refs_12_), channel_id=1, source_target_pairs={{0,1},{1,0},{2,3},{3,2},{4,5},{5,4},{6,7},{7,6},{8,9},{9,8},{10,11... | collective-permute-start | bytes 3145736 | tf_op jit(solution)/shard_map/ppermute | solution.py:26
  90.1 24.6 %collective-permute-start.18 = (bf16[512,256]{1,0:T(8,128)(2,1)S(1)}, bf16[512,256]{1,0:T(8,128)(2,1)S(1)}, u32[]{:S(2)}, u32[]{:S(2)}) collective-permute-start(bf16[512,256]{1,0:T(8,128)(2,1)S(1)} %fusion.1), channel_id=1, source_target_pairs={{0,8},{1,9},{2,10},{3,11},{4,12},{5,13},{6,14},{7,15},{8,0},{9,1},... | collective-permute-start | bytes 786440 | tf_op jit(solution)/shard_map/ppermute | solution.py:26
  95.9 19.9 %collective-permute-start.27 = (bf16[1024,128]{1,0:T(8,128)(2,1)S(1)}, bf16[1024,128]{1,0:T(8,128)(2,1)S(1)}, u32[]{:S(2)}, u32[]{:S(2)}) collective-permute-start(bf16[1024,128]{1,0:T(8,128)(2,1)S(1)} %get-tuple-element.40), channel_id=1, source_target_pairs={{0,13},{1,12},{2,15},{3,14},{4,9},{5,8},{6,11},{7,10},{8,5},{9,4},... | collective-permute-start | bytes 786440 | tf_op jit(solution)/shard_map/ppermute | solution.py:26
  98.2 24.6 %collective-permute-start.28 = (bf16[1024,128]{1,0:T(8,128)(2,1)S(1)}, bf16[1024,128]{1,0:T(8,128)(2,1)S(1)}, u32[]{:S(2)}, u32[]{:S(2)}) collective-permute-start(bf16[1024,128]{1,0:T(8,128)(2,1)S(1)} %get-tuple-element.41), channel_id=1, source_target_pairs={{0,2},{1,3},{2,0},{3,1},{4,6},{5,7},{6,4},{7,5},{8,10},{9,11},{10,... | collective-permute-start | bytes 786440 | tf_op jit(solution)/shard_map/ppermute | solution.py:26
  100.4 24.4 %collective-permute-start.29 = (bf16[1024,128]{1,0:T(8,128)(2,1)S(1)}, bf16[1024,128]{1,0:T(8,128)(2,1)S(1)}, u32[]{:S(2)}, u32[]{:S(2)}) collective-permute-start(bf16[1024,128]{1,0:T(8,128)(2,1)S(1)} %get-tuple-element.42), channel_id=1, source_target_pairs={{0,10},{1,11},{2,8},{3,9},{4,14},{5,15},{6,12},{7,13},{8,2},{9,3},... | collective-permute-start | bytes 786440 | tf_op jit(solution)/shard_map/ppermute | solution.py:26
  114.7 36.4 %collective-permute-start.13 = (bf16[512,1024]{1,0:T(8,128)(2,1)S(1)}, bf16[512,1024]{1,0:T(8,128)(2,1)S(1)}, u32[]{:S(2)}, u32[]{:S(2)}) collective-permute-start(bf16[512,1024]{1,0:T(8,128)(2,1)S(1)} %constant_dynamic-update-slice_fusion.refs_12_), channel_id=1, source_target_pairs={{0,2},{1,3},{2,0},{3,1},{4,6},{5,7},{6,4},{7,5},{8,10},{9,11},{10,... | collective-permute-start | bytes 3145736 | tf_op jit(solution)/shard_map/ppermute | solution.py:26
  116.5 16.5 %collective-permute-start.30 = (bf16[1024,128]{1,0:T(8,128)(2,1)S(1)}, bf16[1024,128]{1,0:T(8,128)(2,1)S(1)}, u32[]{:S(2)}, u32[]{:S(2)}) collective-permute-start(bf16[1024,128]{1,0:T(8,128)(2,1)S(1)} %get-tuple-element.43), channel_id=1, source_target_pairs={{0,6},{1,7},{2,4},{3,5},{4,2},{5,3},{6,0},{7,1},{8,14},{9,15},{10,... | collective-permute-start | bytes 786440 | tf_op jit(solution)/shard_map/ppermute | solution.py:26
  123.5 13.1 %collective-permute-start.31 = (bf16[1024,128]{1,0:T(8,128)(2,1)S(1)}, bf16[1024,128]{1,0:T(8,128)(2,1)S(1)}, u32[]{:S(2)}, u32[]{:S(2)}) collective-permute-start(bf16[1024,128]{1,0:T(8,128)(2,1)S(1)} %get-tuple-element.44), channel_id=1, source_target_pairs={{0,14},{1,15},{2,12},{3,13},{4,10},{5,11},{6,8},{7,9},{8,6},{9,7},... | collective-permute-start | bytes 786440 | tf_op jit(solution)/shard_map/ppermute | solution.py:26
  124.8 19.8 %collective-permute-start.19 = (bf16[512,256]{1,0:T(8,128)(2,1)S(1)}, bf16[512,256]{1,0:T(8,128)(2,1)S(1)}, u32[]{:S(2)}, u32[]{:S(2)}) collective-permute-start(bf16[512,256]{1,0:T(8,128)(2,1)S(1)} %fusion), channel_id=1, source_target_pairs={{0,4},{1,5},{2,6},{3,7},{4,0},{5,1},{6,2},{7,3},{8,12},{9,13},{10,... | collective-permute-start | bytes 786440 | tf_op jit(solution)/shard_map/ppermute | solution.py:26
  133.1 18.9 %collective-permute-start.21 = (bf16[1024,128]{1,0:T(8,128)(2,1)S(1)}, bf16[1024,128]{1,0:T(8,128)(2,1)S(1)}, u32[]{:S(2)}, u32[]{:S(2)}) collective-permute-start(bf16[1024,128]{1,0:T(8,128)(2,1)S(1)} %get-tuple-element.34), channel_id=1, source_target_pairs={{0,8},{1,9},{2,10},{3,11},{4,12},{5,13},{6,14},{7,15},{8,0},{9,1},... | collective-permute-start | bytes 786440 | tf_op jit(solution)/shard_map/ppermute | solution.py:26
  136.6 23.2 %collective-permute-start.22 = (bf16[1024,128]{1,0:T(8,128)(2,1)S(1)}, bf16[1024,128]{1,0:T(8,128)(2,1)S(1)}, u32[]{:S(2)}, u32[]{:S(2)}) collective-permute-start(bf16[1024,128]{1,0:T(8,128)(2,1)S(1)} %get-tuple-element.35), channel_id=1, source_target_pairs={{0,4},{1,5},{2,6},{3,7},{4,0},{5,1},{6,2},{7,3},{8,12},{9,13},{10,... | collective-permute-start | bytes 786440 | tf_op jit(solution)/shard_map/ppermute | solution.py:26
  144.6 15.9 %collective-permute-start.23 = (bf16[1024,128]{1,0:T(8,128)(2,1)S(1)}, bf16[1024,128]{1,0:T(8,128)(2,1)S(1)}, u32[]{:S(2)}, u32[]{:S(2)}) collective-permute-start(bf16[1024,128]{1,0:T(8,128)(2,1)S(1)} %get-tuple-element.36), channel_id=1, source_target_pairs={{0,12},{1,13},{2,14},{3,15},{4,8},{5,9},{6,10},{7,11},{8,4},{9,5},... | collective-permute-start | bytes 786440 | tf_op jit(solution)/shard_map/ppermute | solution.py:26
  146.9 16.3 %collective-permute-start = (bf16[1024,128]{1,0:T(8,128)(2,1)S(1)}, bf16[1024,128]{1,0:T(8,128)(2,1)S(1)}, u32[]{:S(2)}, u32[]{:S(2)}) collective-permute-start(bf16[1024,128]{1,0:T(8,128)(2,1)S(1)} %get-tuple-element.24), channel_id=1, source_target_pairs={{0,3},{1,2},{2,1},{3,0},{4,7},{5,6},{6,5},{7,4},{8,11},{9,10},{10,... | collective-permute-start | bytes 786440 | tf_op jit(solution)/shard_map/ppermute | solution.py:26
  151.1 19.4 %collective-permute-start.1 = (bf16[1024,128]{1,0:T(8,128)(2,1)S(1)}, bf16[1024,128]{1,0:T(8,128)(2,1)S(1)}, u32[]{:S(2)}, u32[]{:S(2)}) collective-permute-start(bf16[1024,128]{1,0:T(8,128)(2,1)S(1)} %get-tuple-element.25), channel_id=1, source_target_pairs={{0,11},{1,10},{2,9},{3,8},{4,15},{5,14},{6,13},{7,12},{8,3},{9,2},... | collective-permute-start | bytes 786440 | tf_op jit(solution)/shard_map/ppermute | solution.py:26
  152.6 18.8 %collective-permute-start.32 = (bf16[512,256]{1,0:T(8,128)(2,1)S(1)}, bf16[512,256]{1,0:T(8,128)(2,1)S(1)}, u32[]{:S(2)}, u32[]{:S(2)}) collective-permute-start(bf16[512,256]{1,0:T(8,128)(2,1)S(1)} %add_convert_fusion.refs_15_), channel_id=1, source_target_pairs={{0,1},{1,0},{2,3},{3,2},{4,5},{5,4},{6,7},{7,6},{8,9},{9,8},{10,11... | collective-permute-start | bytes 786440 | tf_op jit(solution)/shard_map/ppermute | solution.py:26
  160.5 26.3 %collective-permute-start.33 = (bf16[512,256]{1,0:T(8,128)(2,1)S(1)}, bf16[512,256]{1,0:T(8,128)(2,1)S(1)}, u32[]{:S(2)}, u32[]{:S(2)}) collective-permute-start(bf16[512,256]{1,0:T(8,128)(2,1)S(1)} %add_convert_fusion.refs_15_), channel_id=1, source_target_pairs={{0,2},{1,3},{2,0},{3,1},{4,6},{5,7},{6,4},{7,5},{8,10},{9,11},{10,... | collective-permute-start | bytes 786440 | tf_op jit(solution)/shard_map/ppermute | solution.py:26
  161.2 42.0 %collective-permute-start.12 = (bf16[512,512]{1,0:T(8,128)(2,1)}, bf16[512,512]{1,0:T(8,128)(2,1)}, u32[]{:S(2)}, u32[]{:S(2)}) collective-permute-start(bf16[512,512]{1,0:T(8,128)(2,1)} %slice.44), channel_id=1, source_target_pairs={{0,2},{1,3},{2,0},{3,1},{4,6},{5,7},{6,4},{7,5},{8,10},{9,11},{10,... | collective-permute-start | bytes 1572872 | tf_op jit(solution)/shard_map/ppermute | solution.py:26
  163.9 39.3 %collective-permute-start.14 = (bf16[512,512]{1,0:T(8,128)(2,1)}, bf16[512,512]{1,0:T(8,128)(2,1)}, u32[]{:S(2)}, u32[]{:S(2)}) collective-permute-start(bf16[512,512]{1,0:T(8,128)(2,1)} %slice.45), channel_id=1, source_target_pairs={{0,1},{1,0},{2,3},{3,2},{4,5},{5,4},{6,7},{7,6},{8,9},{9,8},{10,11... | collective-permute-start | bytes 1572872 | tf_op jit(solution)/shard_map/ppermute | solution.py:26
  171.2 32.0 %collective-permute-start.2 = (bf16[1024,128]{1,0:T(8,128)(2,1)}, bf16[1024,128]{1,0:T(8,128)(2,1)}, u32[]{:S(2)}, u32[]{:S(2)}) collective-permute-start(bf16[1024,128]{1,0:T(8,128)(2,1)} %get-tuple-element.26), channel_id=1, source_target_pairs={{0,7},{1,6},{2,5},{3,4},{4,3},{5,2},{6,1},{7,0},{8,15},{9,14},{10,... | collective-permute-start | bytes 786440 | tf_op jit(solution)/shard_map/ppermute | solution.py:26
  172.2 31.1 %collective-permute-start.3 = (bf16[1024,128]{1,0:T(8,128)(2,1)}, bf16[1024,128]{1,0:T(8,128)(2,1)}, u32[]{:S(2)}, u32[]{:S(2)}) collective-permute-start(bf16[1024,128]{1,0:T(8,128)(2,1)} %get-tuple-element.27), channel_id=1, source_target_pairs={{0,15},{1,14},{2,13},{3,12},{4,11},{5,10},{6,9},{7,8},{8,7},{9,6},... | collective-permute-start | bytes 786440 | tf_op jit(solution)/shard_map/ppermute | solution.py:26
  187.6 15.7 %collective-permute-start.20 = (bf16[512,256]{1,0:T(8,128)(2,1)S(1)}, bf16[512,256]{1,0:T(8,128)(2,1)}, u32[]{:S(2)}, u32[]{:S(2)}) collective-permute-start(bf16[512,256]{1,0:T(8,128)(2,1)S(1)} %add_convert_fusion.refs_15_), channel_id=1, source_target_pairs={{0,3},{1,2},{2,1},{3,0},{4,7},{5,6},{6,5},{7,4},{8,11},{9,10},{10,... | collective-permute-start | bytes 786440 | tf_op jit(solution)/shard_map/ppermute | solution.py:26
  206.7 18.1 %collective-permute-start.34 = (bf16[512,1280]{1,0:T(8,128)(2,1)}, bf16[512,1280]{1,0:T(8,128)(2,1)}, u32[]{:S(2)}, u32[]{:S(2)}) collective-permute-start(bf16[512,1280]{1,0:T(8,128)(2,1)} %weight_grad.7), channel_id=1, source_target_pairs={{0,16},{16,0},{1,17},{17,1},{2,18},{18,2},{3,19},{19,3},{4,20},{20... | collective-permute-start | bytes 3932168 | tf_op jit(solution)/shard_map/ppermute | solution.py:388
  (57 other events, 135.5 us)
